TPU v7x, 32 devices: a whole 2x2x4 slice. The times are simulated.
32 devices in a mesh: dp: 4 (over y, x), seq: 2 (over core), stream: 4 (over z).
Axes of the slice: x: 2, y: 2, z: 4, core: 2. Of those that a mesh axis runs over, the one named last changes fastest.
Arguments:
- tokens: bfloat16 [4096, 6144], P(('dp', 'seq', 'stream')), parts along dimension 0, may hold values from -800 to 800
- norm_gain: float32 [6144], replicated, may hold values from 0.25 to 1.75
- qkv_weight: bfloat16 [3, 6144, 3072], P(None, None, 'stream'), may hold values from -0.08930431 to 0.08930431
- query_gain: float32 [24, 128], P('stream'), may hold values from 0.4 to 6, as said below
- key_gain: float32 [24, 128], P('stream'), may hold values from 0.4 to 6, as said below
- out_weight: bfloat16 [3072, 6144], P('stream'), may hold values from -0.4375 to 0.4375
Outputs:
- attn_branch: bfloat16 [4096, 6144], P(('dp', 'seq', 'stream')), parts along dimension 0
There are 4 independent parts, one for each index of `dp`. A program takes and returns all parts, laid end to end along the dimension named above; an argument that names none is the same for every part. Nothing has to cross between parts.
Inputs may be any that keep to these rules, and one draw needn't show every extreme that they name: `query_gain`: positive. `key_gain`: positive.
All inputs are finite; a program needn't handle non-finite values.
Results may differ from a plain program's by a relative error of at most 0.014.
Values may be sent and summed in bfloat16 or wider, within the bound.
A program may use at most 192 MiB of HBM per device.

v0:
```python
import jax
import jax.numpy as jnp
from jax import lax
from jax.sharding import PartitionSpec as P


def head_layer_norm(raw_proj, gain):
    local_heads = gain.shape[0]
    head_size = gain.shape[1]
    shaped = raw_proj.reshape(raw_proj.shape[0], local_heads, head_size)
    head_mean = jnp.mean(shaped, axis=-1, keepdims=True)
    centred = shaped - head_mean
    head_var = jnp.mean(centred * centred, axis=-1, keepdims=True)
    return (centred * lax.rsqrt(head_var + 1e-06) * gain[None, :, :]).astype(jnp.bfloat16)


def attend_block(running, pieces, queries, scaling):
    peak, total, accum = running
    keys_now, values_now = pieces
    scores = (
        jnp.einsum("qhd,khd->qhk", queries, keys_now, preferred_element_type=jnp.float32) * scaling
    )
    new_peak = jnp.maximum(peak, jnp.max(scores, axis=-1))
    probs = jnp.exp(scores - new_peak[..., None])
    total = jnp.sum(probs, axis=-1)
    weighted = jnp.einsum(
        "qhk,khd->qhd", probs.astype(jnp.bfloat16), values_now, preferred_element_type=jnp.float32
    )
    accum = weighted
    return (new_peak, total, accum)


def on_device(tokens, norm_gain, qkv_weight, query_gain, key_gain, out_weight):
    inputs = tokens.astype(jnp.float32)
    row_mean = jnp.mean(inputs, axis=-1, keepdims=True)
    centred = inputs - row_mean
    row_var = jnp.mean(centred * centred, axis=-1, keepdims=True)
    normed = (centred * lax.rsqrt(row_var + 1e-06) * norm_gain[None, :]).astype(jnp.bfloat16)
    local_heads = query_gain.shape[0]
    head_size = query_gain.shape[1]
    own_rows = tokens.shape[0]
    half_rows = own_rows * lax.axis_size("stream")
    scaling = 1.0 / float(head_size) ** 0.5
    whole = lax.all_gather(normed, ("seq", "stream"), axis=0, tiled=True)
    first_row = lax.axis_index("seq") * half_rows
    own_half = lax.dynamic_slice_in_dim(whole, first_row, half_rows, 0)
    queries = head_layer_norm(
        jnp.dot(own_half, qkv_weight[0], preferred_element_type=jnp.float32), query_gain
    )
    key_value = jnp.einsum("nd,cdk->cnk", whole, qkv_weight[1:], preferred_element_type=jnp.float32)
    keys_all = head_layer_norm(key_value[0], key_gain)
    values_all = key_value[1].astype(jnp.bfloat16).reshape(whole.shape[0], local_heads, head_size)
    initial = (
        jnp.full((half_rows, local_heads), -1e30, jnp.float32),
        jnp.zeros((half_rows, local_heads), jnp.float32),
        jnp.zeros((half_rows, local_heads, head_size), jnp.float32),
    )
    running = attend_block(initial, (keys_all, values_all), queries, scaling)
    peak, total, accum = running
    attended = (
        (accum / total[..., None]).reshape(half_rows, local_heads * head_size).astype(jnp.bfloat16)
    )
    return lax.psum_scatter(
        jnp.dot(attended, out_weight, preferred_element_type=jnp.float32).astype(jnp.bfloat16),
        "stream",
        scatter_dimension=0,
        tiled=True,
    )


def solution(mesh):
    placed = (
        P(("dp", "seq", "stream"), None),
        P(),
        P(None, None, "stream"),
        P("stream", None),
        P("stream", None),
        P("stream", None),
    )
    return jax.shard_map(
        on_device,
        mesh=mesh,
        in_specs=placed,
        out_specs=P(("dp", "seq", "stream"), None),
        check_vma=False,
    )
```

profile of v0, /device:TPU:0, one launch (start us, length us, event | category | flops | bytes accessed | tf_op | source)
XLA Modules:
  0.0 312.6 jit_solution(18396031868714705997)
XLA Ops:
  6.5 0.0 copy-start.1
  6.5 0.0 copy-start.5
  6.5 0.0 all-gather.2.cloned.1.call-start
  6.5 1.8 convert_reduce_fusion
  8.4 2.0 fusion.15
  10.4 0.0 copy-done.1
  10.4 0.0 copy-done.5
  10.4 1.7 fusion.17
  12.1 0.0 all-gather.2.cloned.1.call-update
  12.1 0.0 reduce-scatter.2.cloned.1.call-start
  12.1 7.9 %slice_bitcast_fusion = bf16[768,6144]{0,1:T(8,128)(2,1)} fusion(bf16[3,6144,768]{2,1,0:T(8,128)(2,1)} %param.8), kind=kLoop, calls=%fused_computation.8 | loop fusion | bytes 18874368 | tf_op jit(solution)/shard_map/dot_general | solution.py:48
  20.0 12.8 %copy.9 = bf16[768,6144]{1,0:T(8,128)(2,1)} copy(bf16[768,6144]{0,1:T(8,128)(2,1)} %slice_bitcast_fusion) | data formatting | bytes 18874368 | tf_op jit(solution)/shard_map/dot_general | solution.py:48
  32.8 98.8 %all-gather.2.cloned.1.call-done = bf16[1024,6144]{1,0:T(8,128)(2,1)} async-done(((bf16[128,6144]{1,0:T(8,128)(2,1)}), bf16[1024,6144]{1,0:T(8,128)(2,1)}) %all-gather.2.cloned.1.call-update) | async-done | bytes 12582928 | tf_op jit(solution)/shard_map/all_gather | solution.py:44
  131.7 25.2 %fusion.18 = f32[2,1024,768]{1,2,0:T(8,128)S(1)} fusion(bf16[3,6144,768]{2,1,0:T(8,128)(2,1)} %param.8, bf16[1024,6144]{1,0:T(8,128)(2,1)} %all-gather.2.cloned.1.call-done), kind=kOutput, calls=%fused_computation.26 | convolution fusion | flops 19327352832 | bytes 37748736 | tf_op jit(solution)/shard_map/nd,cdk->cnk/dot_general | solution.py:50
  156.9 0.0 copy-start.2
  156.9 0.2 slice.18
  157.1 1.4 slice.25
  158.5 2.6 copy-done.2
  161.1 7.4 %fusion.35 = (f32[512,6]{0,1:T(8,128)S(1)}, f32[512,6,128]{0,2,1:T(8,128)S(1)}) fusion(bf16[6,128,6144]{2,1,0:T(8,128)(2,1)S(1)} %bitcast.42, bf16[1024,6144]{1,0:T(8,128)(2,1)} %all-gather.2.cloned.1.call-done, s32[]{:T(128)S(6)} %select_n.3), kind=kOutput, calls=%fused_computation.47 | convolution fusion | flops 4832228352 | bytes 17313796 | tf_op jit(solution)/shard_map/dot_general | solution.py:48
  168.6 0.0 copy-start.3
  168.6 1.1 copy-done.3
  169.7 0.2 multiply_reduce_fusion.1
  169.9 2.4 copy.8
  172.3 0.0 copy-start.6
  172.3 0.0 copy-start.7
  172.3 0.3 reduce_sum.65
  172.6 0.0 copy-start
  172.6 3.4 %multiply_reduce_fusion = f32[1024,6]{0,1:T(8,128)S(1)} fusion(f32[1024,6,128]{2,0,1:T(8,128)} %copy.8, f32[1024,6]{0,1:T(8,128)S(1)} %broadcast_multiply_fusion), kind=kLoop, calls=%fused_computation.25 | loop fusion | flops 2353152 | bytes 3194880 | tf_op jit(solution)/shard_map/reduce_sum | solution.py:13
  176.0 0.0 copy-done.6
  176.0 0.0 copy-done.7
  176.1 0.0 copy-done
  176.1 5.2 %bitcast_reduce_fusion = (f32[512,6]{0,1:T(8,128)S(1)}, f32[6,1024,512]{2,1,0:T(8,128)S(1)}) fusion(f32[512,6,128]{0,2,1:T(8,128)} %copy-done.3, f32[6,128]{1,0:T(8,128)S(1)} %copy-done.6, f32[512,6]{0,1:T(8,128)S(1)} %add_rsqrt_fusion.1, f32[512,6]{0,1:T(8,128)S(1)} %broadcast_multiply_fusion.1, f32[1024,6,128]{2,0,1:T(8,128)S(1)} %copy-done, ...), kind=kOutput, calls=%fused_computation.3 | convolution fusion | flops 816313344 | bytes 17393664 | tf_op jit(solution)/shard_map/qhd,khd->qhk/dot_general | solution.py:21
  181.3 0.0 copy-start.4
  181.3 2.1 fusion.4
  183.3 0.0 copy-done.4
  183.4 2.5 fusion.24
  185.9 10.7 %convolution_convert_fusion = bf16[512,6144]{1,0:T(8,128)(2,1)} fusion(bf16[512,768]{0,1:T(8,128)(2,1)S(1)} %bitcast.44, bf16[768,6144]{1,0:T(8,128)(2,1)} %param.11), kind=kOutput, calls=%fused_computation.9 | convolution fusion | flops 4834983936 | bytes 16515072 | tf_op jit(solution)/shard_map/dot_general | solution.py:64
  196.6 0.0 reduce-scatter.2.cloned.1.call-update
  196.6 109.1 %reduce-scatter.2.cloned.1.call-done = bf16[128,6144]{1,0:T(8,128)(2,1)} async-done(((bf16[512,6144]{1,0:T(8,128)(2,1)}), bf16[128,6144]{1,0:T(8,128)(2,1)}) %reduce-scatter.2.cloned.1.call-update) | async-done | bytes 1572880 | tf_op jit(solution)/shard_map/reduce_scatter | solution.py:63
  (7 shorter events, 0.1 us)
Async XLA Ops:
  6.5 3.8 %copy-start.1 = (bf16[128,6144]{1,0:T(8,128)(2,1)S(1)}, bf16[128,6144]{1,0:T(8,128)(2,1)}, u32[]{:S(2)}) copy-start(bf16[128,6144]{1,0:T(8,128)(2,1)} %param.6) | copy-start | bytes 4718596
  6.5 3.8 %copy-start.5 = (f32[6144]{0:T(1024)S(1)}, f32[6144]{0:T(1024)}, u32[]{:S(2)}) copy-start(f32[6144]{0:T(1024)} %param.7) | copy-start | bytes 73732
  6.5 125.1 %all-gather.2.cloned.1.call-start = ((), (), s32[]{:S(2)}) async-start(), calls=%async_computation.1 | async-start | bytes 14155776 | tf_op jit(solution)/shard_map/all_gather | solution.py:44
  12.1 293.6 %reduce-scatter.2.cloned.1.call-start = ((), (), s32[]{:S(2)}) async-start(), calls=%async_computation.2 | async-start | bytes 7864320 | tf_op jit(solution)/shard_map/reduce_scatter | solution.py:63
  156.9 4.2 %copy-start.2 = (bf16[768,6144]{1,0:T(8,128)(2,1)S(1)}, bf16[768,6144]{1,0:T(8,128)(2,1)}, u32[]{:S(2)}) copy-start(bf16[768,6144]{1,0:T(8,128)(2,1)} %copy.9) | copy-start | bytes 28311556
  168.6 1.1 copy-start.3
  172.3 3.7 %copy-start.6 = (f32[6,128]{1,0:T(8,128)S(1)}, f32[6,128]{1,0:T(8,128)}, u32[]{:S(2)}) copy-start(f32[6,128]{1,0:T(8,128)} %param.9) | copy-start | bytes 9220
  172.3 3.8 %copy-start.7 = (f32[6,128]{1,0:T(8,128)S(1)}, f32[6,128]{1,0:T(8,128)}, u32[]{:S(2)}) copy-start(f32[6,128]{1,0:T(8,128)} %param.10) | copy-start | bytes 9220
  172.6 3.5 %copy-start = (f32[1024,6,128]{2,0,1:T(8,128)S(1)}, f32[1024,6,128]{2,0,1:T(8,128)}, u32[]{:S(2)}) copy-start(f32[1024,6,128]{2,0,1:T(8,128)} %copy.8) | copy-start | bytes 9437188
  181.3 2.1 copy-start.4
Sparse Core Ops, SparseCore 0:
  12.2 119.4 all-gather.1
  196.7 108.9 reduce-scatter.1
where the time goes:
time: 313 us
  waiting for transfers between devices  208 us (66%)
  matrix products  51 us (16%)
  local copies, waits for them, and re-layouts  28.4 us (9%)
  between operations  13.6 us (4%)
  other arithmetic  11.5 us (4%)
    reduce_scatter x1, waiting for transfers between devices, on_device(): lax.psum_scatter(jnp.dot(attended, out_weight, preferred_element_type=jnp...  109 us
    all_gather x1, waiting for transfers between devices, on_device(): whole = lax.all_gather(normed, ('seq', 'stream'), axis=0, tiled=True)  98.8 us
    dot_general x1, matrix products, on_device(): jnp.einsum('nd,cdk->cnk', whole, qkv_weight[1:], preferred_element_type=j...  25.2 us
    dot_general x2, local copies, waits for them, and re-layouts, on_device(): jnp.dot(own_half, qkv_weight[0], preferred_element_type=jnp.float32)  20.7 us
    dot_general x1, matrix products, on_device(): jnp.dot(attended, out_weight, preferred_element_type=jnp.float32)  10.7 us
    dot_general x1, matrix products, on_device(): jnp.dot(own_half, qkv_weight[0], preferred_element_type=jnp.float32)  7.4 us
  transfers between devices with their start and end apart: 2, of which 2 were waited for; matrix products, arithmetic and copies ran while one was open for 7% of the time, Pallas kernels for 0%

commit v1 on v0

v1 whole, which is shorter than its diff:
```python
import jax
import jax.numpy as jnp
from jax import lax
from jax.sharding import PartitionSpec as P


def head_layer_norm(raw_proj, gain):
    local_heads = gain.shape[0]
    head_size = gain.shape[1]
    shaped = raw_proj.reshape(raw_proj.shape[0], local_heads, head_size)
    head_mean = jnp.mean(shaped, axis=-1, keepdims=True)
    centred = shaped - head_mean
    head_var = jnp.mean(centred * centred, axis=-1, keepdims=True)
    return (centred * lax.rsqrt(head_var + 1e-06) * gain[None, :, :]).astype(jnp.bfloat16)


def attend(queries, keys, values, scaling):
    scores = (
        jnp.einsum("qhd,khd->qhk", queries, keys, preferred_element_type=jnp.float32) * scaling
    )
    peak = jnp.max(scores, axis=-1, keepdims=True)
    probs = jnp.exp(scores - peak)
    total = jnp.sum(probs, axis=-1)
    weighted = jnp.einsum(
        "qhk,khd->qhd", probs.astype(jnp.bfloat16), values, preferred_element_type=jnp.float32
    )
    return (weighted / total[..., None]).astype(jnp.bfloat16)


def on_device(tokens, norm_gain, qkv_weight, query_gain, key_gain, out_weight):
    inputs = tokens.astype(jnp.float32)
    row_mean = jnp.mean(inputs, axis=-1, keepdims=True)
    centred = inputs - row_mean
    row_var = jnp.mean(centred * centred, axis=-1, keepdims=True)
    normed = (centred * lax.rsqrt(row_var + 1e-06) * norm_gain[None, :]).astype(jnp.bfloat16)
    local_heads, head_size = query_gain.shape
    rows = tokens.shape[0]
    width = local_heads * head_size
    count = lax.axis_size("stream")
    place = lax.axis_index("stream")
    cores = lax.axis_size("seq")
    scaling = 1.0 / float(head_size) ** 0.5

    def rightward(value, first, last):
        return lax.ppermute(value, "stream", [(i, i + 1) for i in range(first, last)])

    def leftward(value, first, last):
        return lax.ppermute(value, "stream", [(i, i - 1) for i in range(first, last, -1)])

    from_left, from_right = [normed], [normed]
    for step in range(1, count):
        from_left.append(rightward(from_left[-1], step - 1, count - 1))
        from_right.append(leftward(from_right[-1], count - step, 0))

    def either(step):
        return jnp.where(place >= step, from_left[step], from_right[step])

    half = count // 2
    longest = jnp.maximum(place, count - 1 - place)
    slots = [(normed, place)]
    for step in range(1, half + 1):
        if step < count:
            slots.append((either(step), jnp.where(place >= step, place - step, place + step)))
    for extra in range(1, count - half):
        step, other = half + extra, half - extra
        far = longest >= step
        slots.append(
            (
                jnp.where(far, either(step), from_right[other]),
                jnp.where(
                    far,
                    jnp.where(place >= step, place - step, place + step),
                    place + other,
                ),
            )
        )

    queries = jnp.zeros((count * rows, local_heads, head_size), jnp.bfloat16)
    keys, values = [], []
    for shard, origin in slots:
        raw = jnp.einsum("nd,cdk->cnk", shard, qkv_weight, preferred_element_type=jnp.float32)
        queries = lax.dynamic_update_slice_in_dim(
            queries, head_layer_norm(raw[0], query_gain), origin * rows, 0
        )
        key_now = head_layer_norm(raw[1], key_gain)
        value_now = raw[2].astype(jnp.bfloat16)
        both = jnp.concatenate([key_now.reshape(rows, width), value_now], axis=1)
        held = [both]
        for turn in range(1, cores):
            held.append(lax.ppermute(both, "seq", [(i, (i + turn) % cores) for i in range(cores)]))
        for piece in held:
            keys.append(piece[:, :width])
            values.append(piece[:, width:])
    keys_all = jnp.concatenate(keys, 0).reshape(-1, local_heads, head_size)
    values_all = jnp.concatenate(values, 0).reshape(-1, local_heads, head_size)

    attended = attend(queries, keys_all, values_all, scaling).reshape(count * rows, width)

    def share(block):
        piece = lax.dynamic_slice_in_dim(attended, block * rows, rows, 0)
        return jnp.dot(piece, out_weight, preferred_element_type=jnp.float32)

    got_left = got_right = None
    for step in range(1, count):
        right_sum = share(lax.rem(place - step + count, count))
        left_sum = share(lax.rem(place + step, count))
        if got_left is not None:
            right_sum = right_sum + got_left
            left_sum = left_sum + got_right
        right_sum, left_sum = lax.optimization_barrier(
            (right_sum.astype(jnp.bfloat16), left_sum.astype(jnp.bfloat16))
        )
        got_left = rightward(right_sum, 0, step)
        got_right = leftward(left_sum, count - 1, count - 1 - step)
    result = share(place)
    if got_left is not None:
        result = result + got_left + got_right
    return result.astype(jnp.bfloat16)


def solution(mesh):
    placed = (
        P(("dp", "seq", "stream"), None),
        P(),
        P(None, None, "stream"),
        P("stream", None),
        P("stream", None),
        P("stream", None),
    )

    return jax.shard_map(
        on_device,
        mesh=mesh,
        in_specs=placed,
        out_specs=P(("dp", "seq", "stream"), None),
        check_vma=False,
    )
```

time: 313 us -> 332 us (1.061)
  waiting for transfers between devices: 208 us -> 137 us
  starting transfers between devices: 0.04 us -> 33.4 us
  other arithmetic: 11.5 us -> 35.7 us
  local copies, waits for them, and re-layouts: 28.4 us -> 52.3 us
  matrix products: 51 us -> 71.7 us
  between operations: 13.6 us -> 0.81 us
    ppermute x0 -> x16, waiting for transfers between devices: none -> 137 us  [the longest x6 81.1 us: rightward(): lax.ppermute(value, 'stream', [(i, i + 1) for i in range(first, last)])]
    reduce_scatter x1 -> x0, waiting for transfers between devices: 109 us -> none  [on_device(): lax.psum_scatter(jnp.dot(attended, out_weight, preferred_element_type=jnp...]
    all_gather x1 -> x0, waiting for transfers between devices: 98.8 us -> none  [on_device(): whole = lax.all_gather(normed, ('seq', 'stream'), axis=0, tiled=True)]
    ppermute x0 -> x16, starting transfers between devices: none -> 33.4 us  [the longest x6 24.5 us: rightward(): lax.ppermute(value, 'stream', [(i, i + 1) for i in range(first, last)])]
    dot_general x2 -> x0, local copies, waits for them, and re-layouts: 20.7 us -> none  [on_device(): jnp.dot(own_half, qkv_weight[0], preferred_element_type=jnp.float32)]
    dot_general x5 -> x10, matrix products: 51 us -> 71.7 us  [the longest x4 49.6 us: on_device(): jnp.einsum('nd,cdk->cnk', shard, qkv_weight, preferred_element_type=jnp.f...]
    slice x2 -> x20, local copies, waits for them, and re-layouts: 1.6 us -> 19.3 us  [the longest x8 8.96 us: on_device(): raw[0]]
    convert_element_type x0 -> x5, other arithmetic: none -> 7.71 us  [the longest x2 5.26 us: head_layer_norm(): (centred * lax.rsqrt(head_var + 1e-06) * gain[None, :, :]).astype(jnp.bfl...]
  transfers between devices with their start and end apart: 2 -> 16, of which waited for: 2 -> 8; matrix products, arithmetic and copies ran while one was open for 7% -> 25% of each run, Pallas kernels for 0% -> 0%
where the time goes in v1:
time: 332 us; the launch traced here: 331 us
  waiting for transfers between devices  137 us (41%)
  matrix products  71.7 us (22%)
  local copies, waits for them, and re-layouts  52.3 us (16%)
  other arithmetic  35.7 us (11%)
  starting transfers between devices  33.4 us (10%)
    ppermute x6, waiting for transfers between devices, rightward(): lax.ppermute(value, 'stream', [(i, i + 1) for i in range(first, last)])  81.1 us
    ppermute x6, waiting for transfers between devices, leftward(): lax.ppermute(value, 'stream', [(i, i - 1) for i in range(first, last, -1)])  55.3 us
    dot_general x4, matrix products, on_device(): jnp.einsum('nd,cdk->cnk', shard, qkv_weight, preferred_element_type=jnp.f...  49.6 us
    ppermute x6, starting transfers between devices, rightward(): lax.ppermute(value, 'stream', [(i, i + 1) for i in range(first, last)])  24.5 us
    dot_general x4, matrix products, share(): return jnp.dot(piece, out_weight, preferred_element_type=jnp.float32)  15.5 us
    unnamed x81, local copies, waits for them, and re-layouts  9.34 us
    slice x8, local copies, waits for them, and re-layouts, on_device(): raw[0]  8.96 us
    ppermute x6, starting transfers between devices, leftward(): lax.ppermute(value, 'stream', [(i, i - 1) for i in range(first, last, -1)])  7.9 us
  transfers between devices with their start and end apart: 16, of which 8 were waited for; matrix products, arithmetic and copies ran while one was open for 25% of the time, Pallas kernels for 0%

profile of v1, /device:TPU:0, one launch (start us, length us, event | category | flops | bytes accessed | tf_op | source)
XLA Modules:
  0.0 330.7 jit_solution(13927606310784753603)
XLA Ops:
  0.0 1.8 convert_reduce_fusion
  3.0 1.3 collective-permute-start.2
  4.3 6.7 %collective-permute-start.1 = (bf16[128,6144]{1,0:T(8,128)(2,1)S(1)}, bf16[128,6144]{1,0:T(8,128)(2,1)}, u32[]{:S(2)}, u32[]{:S(2)}) collective-permute-start(bf16[128,6144]{1,0:T(8,128)(2,1)S(1)} %fusion.11), channel_id=1, source_target_pairs={{0,1},{1,2},{2,3},{4,5},{5,6},{6,7},{8,9},{9,10},{10,11},{12,13},{... | collective-permute-start | bytes 4718600 | tf_op jit(solution)/shard_map/ppermute | solution.py:45
  11.1 11.3 %fusion.31 = f32[3,128,768]{2,1,0:T(8,128)S(1)} fusion(bf16[3,6144,768]{2,1,0:T(8,128)(2,1)} %param.8, bf16[128,6144]{1,0:T(8,128)(2,1)S(1)} %fusion.11), kind=kOutput, calls=%fused_computation.38 | convolution fusion | flops 3623878656 | bytes 31064064 | tf_op jit(solution)/shard_map/nd,cdk->cnk/dot_general | solution.py:81
  25.8 1.1 copy.62
  27.7 0.9 fusion.55
  29.4 14.1 %collective-permute-done.1 = bf16[128,6144]{1,0:T(8,128)(2,1)} collective-permute-done((bf16[128,6144]{1,0:T(8,128)(2,1)S(1)}, bf16[128,6144]{1,0:T(8,128)(2,1)}, u32[]{:S(2)}, u32[]{:S(2)}) %collective-permute-start.1) | collective-permute-done | bytes 1572896 | tf_op jit(solution)/shard_map/ppermute | solution.py:45
  43.6 1.8 collective-permute-start.4
  45.4 1.3 collective-permute-start.5
  46.7 11.8 %fusion.34 = f32[3,128,768]{2,1,0:T(8,128)S(1)} fusion(bf16[3,6144,768]{2,1,0:T(8,128)(2,1)} %param.8, bf16[128,6144]{1,0:T(8,128)(2,1)} %collective-permute-done.1, bf16[128,6144]{1,0:T(8,128)(2,1)} %collective-permute-done.2, pred[]{:T(512)S(6)} %ge.15), kind=kOutput, calls=%fused_computation.39 | convolution fusion | flops 3624665088 | bytes 32636928 | tf_op jit(solution)/shard_map/nd,cdk->cnk/dot_general | solution.py:81
  62.6 1.8 collective-permute-start.7
  64.5 21.8 %collective-permute-done.5 = bf16[128,6144]{1,0:T(8,128)(2,1)} collective-permute-done((bf16[128,6144]{1,0:T(8,128)(2,1)}, bf16[128,6144]{1,0:T(8,128)(2,1)}, u32[]{:S(2)}, u32[]{:S(2)}) %collective-permute-start.5) | collective-permute-done | bytes 1572896 | tf_op jit(solution)/shard_map/ppermute | solution.py:48
  86.2 1.3 collective-permute-start.8
  87.5 12.0 %fusion.37 = f32[3,128,768]{2,1,0:T(8,128)S(1)} fusion(bf16[3,6144,768]{2,1,0:T(8,128)(2,1)} %param.8, bf16[128,6144]{1,0:T(8,128)(2,1)} %collective-permute-done.4, bf16[128,6144]{1,0:T(8,128)(2,1)} %collective-permute-done.5, pred[]{:T(512)S(6)} %ge.16), kind=kOutput, calls=%fused_computation.40 | convolution fusion | flops 3624665088 | bytes 32636928 | tf_op jit(solution)/shard_map/nd,cdk->cnk/dot_general | solution.py:81
  100.4 1.9 copy.41
  102.3 1.9 copy.44
  104.2 1.0 reduce_sum.177
  105.3 1.3 multiply_reduce_fusion.5
  108.0 1.9 copy.46
  110.7 1.9 copy.43
  112.6 1.9 copy.66
  114.6 1.0 reduce_sum.185
  116.2 1.6 multiply_reduce_fusion.1
  117.8 4.8 %collective-permute-done.8 = bf16[128,6144]{1,0:T(8,128)(2,1)} collective-permute-done((bf16[128,6144]{1,0:T(8,128)(2,1)}, bf16[128,6144]{1,0:T(8,128)(2,1)}, u32[]{:S(2)}, u32[]{:S(2)}) %collective-permute-start.8) | collective-permute-done | bytes 1572896 | tf_op jit(solution)/shard_map/ppermute | solution.py:48
  122.6 14.6 %fusion.40 = f32[3,128,768]{2,1,0:T(8,128)} fusion(bf16[3,6144,768]{2,1,0:T(8,128)(2,1)} %param.8, bf16[128,6144]{1,0:T(8,128)(2,1)} %collective-permute-done.2, bf16[128,6144]{1,0:T(8,128)(2,1)} %collective-permute-done.7, bf16[128,6144]{1,0:T(8,128)(2,1)} %collective-permute-done.8, pred[]{:T(512)S(6)} %ge.18, pred[]{:T(512)S(6)} %ge.17), kind=kOutput, calls=%fused_computation.41 | convolution fusion | flops 3625451520 | bytes 34209792 | tf_op jit(solution)/shard_map/nd,cdk->cnk/dot_general | solution.py:81
  137.2 2.0 fusion.80
  139.3 1.9 copy.47
  141.2 1.9 copy.50
  143.1 1.6 reduce_sum.179
  145.4 1.3 multiply_reduce_fusion.4
  148.1 1.9 copy.52
  150.8 1.9 copy.49
  152.7 3.0 fusion.45
  156.6 1.9 copy.68
  158.5 1.6 reduce_sum.187
  160.8 1.0 multiply_reduce_fusion
  162.5 2.2 multiply_convert_fusion
  164.8 1.1 copy.63
  165.9 1.8 fusion.87
  172.0 1.7 fusion.86
  176.3 1.7 fusion.56
  179.0 1.0 fusion.85
  180.1 1.1 constant_dynamic-update-slice_fusion
  182.1 0.9 fusion.57
  184.1 1.6 fusion.58
  185.7 1.0 fusion.84
  186.8 1.6 copy.53
  189.5 3.2 bitcast_reduce_fusion
  192.7 2.6 fusion.1
  195.4 3.4 %fusion.12 = bf16[512,6,128]{0,2,1:T(8,128)(2,1)S(1)} fusion(bf16[1024,6,128]{0,2,1:T(8,128)(2,1)S(1)} %bitcast.146, f32[6,1024,512]{2,1,0:T(8,128)S(1)} %get-tuple-element.52, f32[512,6]{0,1:T(8,128)S(1)} %get-tuple-element.51, f32[512,6]{0,1:T(8,128)} %fusion.1), kind=kOutput, calls=%fused_computation.21 | convolution fusion | flops 815529984 | bytes 14966784 | tf_op jit(solution)/shard_map/qhk,khd->qhd/dot_general | solution.py:24
  198.8 3.7 %fusion.89 = (bf16[128,6144]{1,0:T(8,128)(2,1)}, f32[128,6144]{1,0:T(8,128)}) fusion(bf16[768,6144]{1,0:T(8,128)(2,1)S(1)} %bitcast.123, bf16[512,768]{0,1:T(8,128)(2,1)S(1)} %bitcast.155, s32[]{:T(128)S(6)} %select_n.80), kind=kOutput, calls=%fused_computation.146 | convolution fusion | flops 1208745984 | bytes 14352388 | tf_op jit(solution)/shard_map/dot_general | solution.py:101
  202.5 2.7 fusion.88
  205.2 1.9 collective-permute-start.11
  207.0 3.1 collective-permute-start.10
  210.1 33.3 %collective-permute-done.10 = bf16[128,6144]{1,0:T(8,128)(2,1)} collective-permute-done((bf16[128,6144]{1,0:T(8,128)(2,1)}, bf16[128,6144]{1,0:T(8,128)(2,1)}, u32[]{:S(2)}, u32[]{:S(2)}) %collective-permute-start.10) | collective-permute-done | bytes 1572896 | tf_op jit(solution)/shard_map/ppermute | solution.py:45
  243.4 6.7 %add_convert_fusion.3 = (bf16[128,6144]{1,0:T(8,128)(2,1)S(1)}, bf16[128,6144]{1,0:T(8,128)(2,1)S(1)}) fusion(bf16[128,6144]{1,0:T(8,128)(2,1)} %collective-permute-done.11, bf16[128,6144]{1,0:T(8,128)(2,1)} %collective-permute-done.10, bf16[768,6144]{1,0:T(8,128)(2,1)} %param.11, bf16[512,768]{0,1:T(8,128)(2,1)} %bitcast.157, s32[]{:T(128)S(6)} %select_n.81), kind=kOutput, calls=%fused_computation.18 | convolution fusion | flops 1212678144 | bytes 15925252 | tf_op jit(solution)/shard_map/dot_general | solution.py:101
  250.2 4.5 %collective-permute-start.12 = (bf16[128,6144]{1,0:T(8,128)(2,1)S(1)}, bf16[128,6144]{1,0:T(8,128)(2,1)S(1)}, u32[]{:S(2)}, u32[]{:S(2)}) collective-permute-start(bf16[128,6144]{1,0:T(8,128)(2,1)S(1)} %get-tuple-element.13), channel_id=1, source_target_pairs={{0,1},{1,2},{4,5},{5,6},{8,9},{9,10},{12,13},{13,14},{16,17},{17,1... | collective-permute-start | bytes 4718600 | tf_op jit(solution)/shard_map/ppermute | solution.py:45
  255.4 32.5 %collective-permute-done.12 = bf16[128,6144]{1,0:T(8,128)(2,1)S(1)} collective-permute-done((bf16[128,6144]{1,0:T(8,128)(2,1)S(1)}, bf16[128,6144]{1,0:T(8,128)(2,1)S(1)}, u32[]{:S(2)}, u32[]{:S(2)}) %collective-permute-start.12) | collective-permute-done | bytes 1572896 | tf_op jit(solution)/shard_map/ppermute | solution.py:45
  288.6 1.4 collective-permute-start.15
  290.0 6.6 %collective-permute-start.14 = (bf16[128,6144]{1,0:T(8,128)(2,1)S(1)}, bf16[128,6144]{1,0:T(8,128)(2,1)S(1)}, u32[]{:S(2)}, u32[]{:S(2)}) collective-permute-start(bf16[128,6144]{1,0:T(8,128)(2,1)S(1)} %add_convert_fusion.2), channel_id=1, source_target_pairs={{0,1},{1,2},{2,3},{4,5},{5,6},{6,7},{8,9},{9,10},{10,11},{12,13},{... | collective-permute-start | bytes 4718600 | tf_op jit(solution)/shard_map/ppermute | solution.py:45
  296.6 2.4 fusion.69
  299.0 28.7 %collective-permute-done.15 = bf16[128,6144]{1,0:T(8,128)(2,1)S(1)} collective-permute-done((bf16[128,6144]{1,0:T(8,128)(2,1)S(1)}, bf16[128,6144]{1,0:T(8,128)(2,1)S(1)}, u32[]{:S(2)}, u32[]{:S(2)}) %collective-permute-start.15) | collective-permute-done | bytes 1572896 | tf_op jit(solution)/shard_map/ppermute | solution.py:48
  327.8 1.2 collective-permute-done.14
  328.9 1.8 add_convert_fusion
  (165 shorter events, 31.2 us)
Async XLA Ops:
  0.0 1.9 copy-start
  0.0 2.5 copy-start.30
  3.0 42.3 %collective-permute-start.2 = (bf16[128,6144]{1,0:T(8,128)(2,1)S(1)}, bf16[128,6144]{1,0:T(8,128)(2,1)}, u32[]{:S(2)}, u32[]{:S(2)}) collective-permute-start(bf16[128,6144]{1,0:T(8,128)(2,1)S(1)} %fusion.11), channel_id=1, source_target_pairs={{3,2},{2,1},{1,0},{7,6},{6,5},{5,4},{11,10},{10,9},{9,8},{15,14},{... | collective-permute-start | bytes 4718600 | tf_op jit(solution)/shard_map/ppermute | solution.py:48
  4.3 39.2 %collective-permute-start.1 = (bf16[128,6144]{1,0:T(8,128)(2,1)S(1)}, bf16[128,6144]{1,0:T(8,128)(2,1)}, u32[]{:S(2)}, u32[]{:S(2)}) collective-permute-start(bf16[128,6144]{1,0:T(8,128)(2,1)S(1)} %fusion.11), channel_id=1, source_target_pairs={{0,1},{1,2},{2,3},{4,5},{5,6},{6,7},{8,9},{9,10},{10,11},{12,13},{... | collective-permute-start | bytes 4718600 | tf_op jit(solution)/shard_map/ppermute | solution.py:45
  24.8 2.9 copy-start.22
  26.9 18.5 %copy-start.2 = (f32[1,128,768]{1,2,0:T(8,128)}, f32[1,128,768]{1,2,0:T(8,128)S(1)}, u32[]{:S(2)}) copy-start(f32[1,128,768]{1,2,0:T(8,128)S(1)} %copy.62) | copy-start | bytes 1179652
  27.0 0.7 copy-start.27
  43.6 19.1 %collective-permute-start.4 = (bf16[128,6144]{1,0:T(8,128)(2,1)}, bf16[128,6144]{1,0:T(8,128)(2,1)}, u32[]{:S(2)}, u32[]{:S(2)}) collective-permute-start(bf16[128,6144]{1,0:T(8,128)(2,1)} %collective-permute-done.1), channel_id=1, source_target_pairs={{1,2},{2,3},{5,6},{6,7},{9,10},{10,11},{13,14},{14,15},{17,18},{18... | collective-permute-start | bytes 4718600 | tf_op jit(solution)/shard_map/ppermute | solution.py:45
  45.4 40.9 %collective-permute-start.5 = (bf16[128,6144]{1,0:T(8,128)(2,1)}, bf16[128,6144]{1,0:T(8,128)(2,1)}, u32[]{:S(2)}, u32[]{:S(2)}) collective-permute-start(bf16[128,6144]{1,0:T(8,128)(2,1)} %collective-permute-done.2), channel_id=1, source_target_pairs={{2,1},{1,0},{6,5},{5,4},{10,9},{9,8},{14,13},{13,12},{18,17},{17,1... | collective-permute-start | bytes 4718600 | tf_op jit(solution)/shard_map/ppermute | solution.py:48
  58.8 2.9 copy-start.7
  59.2 0.6 copy-start.23
  61.9 24.4 %copy-start.4 = (f32[1,128,768]{1,2,0:T(8,128)}, f32[1,128,768]{1,2,0:T(8,128)S(1)}, u32[]{:S(2)}) copy-start(f32[1,128,768]{1,2,0:T(8,128)S(1)} %copy.64) | copy-start | bytes 1179652
  61.9 24.3 %copy-start.28 = (f32[128,6]{0,1:T(8,128)}, f32[128,6]{0,1:T(8,128)S(1)}, u32[]{:S(2)}) copy-start(f32[128,6]{0,1:T(8,128)S(1)} %broadcast_multiply_fusion.2) | copy-start | bytes 9220
  62.6 55.2 %collective-permute-start.7 = (bf16[128,6144]{1,0:T(8,128)(2,1)}, bf16[128,6144]{1,0:T(8,128)(2,1)}, u32[]{:S(2)}, u32[]{:S(2)}) collective-permute-start(bf16[128,6144]{1,0:T(8,128)(2,1)} %collective-permute-done.4), channel_id=1, source_target_pairs={{2,3},{6,7},{10,11},{14,15},{18,19},{22,23},{26,27},{30,31}} | collective-permute-start | bytes 4718600 | tf_op jit(solution)/shard_map/ppermute | solution.py:45
  86.2 36.3 %collective-permute-start.8 = (bf16[128,6144]{1,0:T(8,128)(2,1)}, bf16[128,6144]{1,0:T(8,128)(2,1)}, u32[]{:S(2)}, u32[]{:S(2)}) collective-permute-start(bf16[128,6144]{1,0:T(8,128)(2,1)} %collective-permute-done.5), channel_id=1, source_target_pairs={{1,0},{5,4},{9,8},{13,12},{17,16},{21,20},{25,24},{29,28}} | collective-permute-start | bytes 4718600 | tf_op jit(solution)/shard_map/ppermute | solution.py:48
  106.6 0.6 copy-start.24
  115.6 0.6 copy-start.29
  146.7 0.6 copy-start.26
  152.7 3.0 copy-start.20
  155.8 6.8 %copy-start.3 = (f32[1,128,768]{1,2,0:T(8,128)S(1)}, f32[1,128,768]{1,2,0:T(8,128)}, u32[]{:S(2)}) copy-start(f32[1,128,768]{1,2,0:T(8,128)} %copy-done.2) | copy-start | bytes 1179652
  155.8 6.8 %copy-start.5 = (f32[1,128,768]{1,2,0:T(8,128)S(1)}, f32[1,128,768]{1,2,0:T(8,128)}, u32[]{:S(2)}) copy-start(f32[1,128,768]{1,2,0:T(8,128)} %copy-done.4) | copy-start | bytes 1179652
  155.8 6.8 %copy-start.6 = (f32[1,128,768]{1,2,0:T(8,128)S(1)}, f32[1,128,768]{1,2,0:T(8,128)}, u32[]{:S(2)}) copy-start(f32[1,128,768]{1,2,0:T(8,128)} %copy.66) | copy-start | bytes 1179652
  156.6 9.3 %collective-permute-start = (bf16[128,1536]{1,0:T(8,128)(2,1)}, bf16[128,1536]{1,0:T(8,128)(2,1)}, u32[]{:S(2)}, u32[]{:S(2)}) collective-permute-start(bf16[128,1536]{1,0:T(8,128)(2,1)} %pad_maximum_fusion), channel_id=1, source_target_pairs={{0,4},{4,0},{1,5},{5,1},{2,6},{6,2},{3,7},{7,3},{8,12},{12,8},{9,1... | collective-permute-start | bytes 1179656 | tf_op jit(solution)/shard_map/ppermute | solution.py:90
  164.8 3.6 %copy-start.16 = (bf16[128,768]{1,0:T(8,128)(2,1)S(1)}, bf16[128,768]{1,0:T(8,128)(2,1)}, u32[]{:S(2)}) copy-start(bf16[128,768]{1,0:T(8,128)(2,1)} %get-tuple-element.48) | copy-start | bytes 589828
  165.9 3.9 %copy-start.19 = (bf16[128,6,128]{0,2,1:T(8,128)(2,1)S(1)}, bf16[128,6,128]{0,2,1:T(8,128)(2,1)}, u32[]{:S(2)}) copy-start(bf16[128,6,128]{0,2,1:T(8,128)(2,1)} %get-tuple-element.44) | copy-start | bytes 589828
  167.7 2.3 copy-start.18
  167.7 2.5 copy-start.17
  169.2 2.1 collective-permute-start.3
  170.4 4.0 %copy-start.15 = (bf16[128,768]{1,0:T(8,128)(2,1)S(1)}, bf16[128,768]{1,0:T(8,128)(2,1)}, u32[]{:S(2)}) copy-start(bf16[128,768]{1,0:T(8,128)(2,1)} %get-tuple-element.49) | copy-start | bytes 589828
  170.7 5.6 %copy-start.8 = (f32[128,6,128]{2,0,1:T(8,128)S(1)}, f32[128,6,128]{2,0,1:T(8,128)}, u32[]{:S(2)}) copy-start(f32[128,6,128]{2,0,1:T(8,128)} %copy-done.7) | copy-start | bytes 1179652
  171.2 0.8 copy-start.21
  174.4 4.6 %copy-start.11 = (bf16[1024,768]{1,0:T(8,128)(2,1)S(1)}, bf16[1024,768]{1,0:T(8,128)(2,1)}, u32[]{:S(2)}) copy-start(bf16[1024,768]{1,0:T(8,128)(2,1)} %get-tuple-element.19) | copy-start | bytes 4718596
  175.2 3.8 %collective-permute-start.6 = (bf16[128,1536]{1,0:T(8,128)(2,1)}, bf16[128,1536]{1,0:T(8,128)(2,1)}, u32[]{:S(2)}, u32[]{:S(2)}) collective-permute-start(bf16[128,1536]{1,0:T(8,128)(2,1)} %pad_maximum_fusion.2), channel_id=1, source_target_pairs={{0,4},{4,0},{1,5},{5,1},{2,6},{6,2},{3,7},{7,3},{8,12},{12,8},{9,1... | collective-permute-start | bytes 1179656 | tf_op jit(solution)/shard_map/ppermute | solution.py:90
  176.3 4.9 %copy-start.14 = (bf16[128,768]{1,0:T(8,128)(2,1)S(1)}, bf16[128,768]{1,0:T(8,128)(2,1)}, u32[]{:S(2)}) copy-start(bf16[128,768]{1,0:T(8,128)(2,1)} %get-tuple-element.47) | copy-start | bytes 589828
  178.1 4.0 %copy-start.9 = (f32[128,6,128]{2,0,1:T(8,128)S(1)}, f32[128,6,128]{2,0,1:T(8,128)}, u32[]{:S(2)}) copy-start(f32[128,6,128]{2,0,1:T(8,128)} %copy.44) | copy-start | bytes 1179652
  178.1 4.0 %copy-start.25 = (f32[128,6]{0,1:T(8,128)S(1)}, f32[128,6]{0,1:T(8,128)}, u32[]{:S(2)}) copy-start(f32[128,6]{0,1:T(8,128)} %copy-done.24) | copy-start | bytes 9220
  180.1 4.0 %copy-start.10 = (f32[128,6,128]{2,0,1:T(8,128)S(1)}, f32[128,6,128]{2,0,1:T(8,128)}, u32[]{:S(2)}) copy-start(f32[128,6,128]{2,0,1:T(8,128)} %copy.50) | copy-start | bytes 1179652
  182.0 3.8 %collective-permute-start.9 = (bf16[128,1536]{1,0:T(8,128)(2,1)}, bf16[128,1536]{1,0:T(8,128)(2,1)}, u32[]{:S(2)}, u32[]{:S(2)}) collective-permute-start(bf16[128,1536]{1,0:T(8,128)(2,1)} %pad_maximum_fusion.3), channel_id=1, source_target_pairs={{0,4},{4,0},{1,5},{5,1},{2,6},{6,2},{3,7},{7,3},{8,12},{12,8},{9,1... | collective-permute-start | bytes 1179656 | tf_op jit(solution)/shard_map/ppermute | solution.py:90
  192.7 2.7 copy-start.12
  192.7 6.1 %slice-start = ((s8[9437184]{0:T(1024)(128)(4,1)}), s8[1048576]{0:T(1024)(128)(4,1)S(1)}, s32[]{:S(2)}) async-start(s8[9437184]{0:T(1024)(128)(4,1)} %bitcast.122), calls=%async_computation | async-start | bytes 2097152
  192.7 6.1 %slice-start.1 = ((s8[9437184]{0:T(1024)(128)(4,1)}), s8[4194304]{0:T(1024)(128)(4,1)S(1)}, s32[]{:S(2)}) async-start(s8[9437184]{0:T(1024)(128)(4,1)} %bitcast.122), calls=%async_computation.1 | async-start | bytes 8388608
  195.4 3.4 %slice-start.2 = ((s8[9437184]{0:T(1024)(128)(4,1)}), s8[4194304]{0:T(1024)(128)(4,1)S(1)}, s32[]{:S(2)}) async-start(s8[9437184]{0:T(1024)(128)(4,1)} %bitcast.122), calls=%async_computation.2 | async-start | bytes 8388608
  198.7 3.7 %copy-start.13 = (bf16[512,6,128]{0,2,1:T(8,128)(2,1)}, bf16[512,6,128]{0,2,1:T(8,128)(2,1)S(1)}, u32[]{:S(2)}) copy-start(bf16[512,6,128]{0,2,1:T(8,128)(2,1)S(1)} %fusion.12) | copy-start | bytes 2359300
  205.2 4.9 %collective-permute-start.11 = (bf16[128,6144]{1,0:T(8,128)(2,1)}, bf16[128,6144]{1,0:T(8,128)(2,1)}, u32[]{:S(2)}, u32[]{:S(2)}) collective-permute-start(bf16[128,6144]{1,0:T(8,128)(2,1)} %get-tuple-element.12), channel_id=1, source_target_pairs={{3,2},{7,6},{11,10},{15,14},{19,18},{23,22},{27,26},{31,30}} | collective-permute-start | bytes 4718600 | tf_op jit(solution)/shard_map/ppermute | solution.py:48
  207.0 36.4 %collective-permute-start.10 = (bf16[128,6144]{1,0:T(8,128)(2,1)}, bf16[128,6144]{1,0:T(8,128)(2,1)}, u32[]{:S(2)}, u32[]{:S(2)}) collective-permute-start(bf16[128,6144]{1,0:T(8,128)(2,1)} %get-tuple-element.11), channel_id=1, source_target_pairs={{0,1},{4,5},{8,9},{12,13},{16,17},{20,21},{24,25},{28,29}} | collective-permute-start | bytes 4718600 | tf_op jit(solution)/shard_map/ppermute | solution.py:45
  243.4 44.4 %copy-start.1 = (f32[128,6144]{1,0:T(8,128)S(1)}, f32[128,6144]{1,0:T(8,128)}, u32[]{:S(2)}) copy-start(f32[128,6144]{1,0:T(8,128)} %get-tuple-element.56) | copy-start | bytes 9437188
  243.4 53.1 %slice-start.3 = ((s8[9437184]{0:T(1024)(128)(4,1)}), s8[1048576]{0:T(1024)(128)(4,1)S(1)}, s32[]{:S(2)}) async-start(s8[9437184]{0:T(1024)(128)(4,1)} %bitcast.124), calls=%async_computation.3 | async-start | bytes 2097152
  243.4 53.1 %slice-start.4 = ((s8[9437184]{0:T(1024)(128)(4,1)}), s8[4194304]{0:T(1024)(128)(4,1)S(1)}, s32[]{:S(2)}) async-start(s8[9437184]{0:T(1024)(128)(4,1)} %bitcast.124), calls=%async_computation.4 | async-start | bytes 8388608
  250.2 37.7 %collective-permute-start.12 = (bf16[128,6144]{1,0:T(8,128)(2,1)S(1)}, bf16[128,6144]{1,0:T(8,128)(2,1)S(1)}, u32[]{:S(2)}, u32[]{:S(2)}) collective-permute-start(bf16[128,6144]{1,0:T(8,128)(2,1)S(1)} %get-tuple-element.13), channel_id=1, source_target_pairs={{0,1},{1,2},{4,5},{5,6},{8,9},{9,10},{12,13},{13,14},{16,17},{17,1... | collective-permute-start | bytes 4718600 | tf_op jit(solution)/shard_map/ppermute | solution.py:45
  254.6 33.5 %collective-permute-start.13 = (bf16[128,6144]{1,0:T(8,128)(2,1)S(1)}, bf16[128,6144]{1,0:T(8,128)(2,1)S(1)}, u32[]{:S(2)}, u32[]{:S(2)}) collective-permute-start(bf16[128,6144]{1,0:T(8,128)(2,1)S(1)} %get-tuple-element.14), channel_id=1, source_target_pairs={{3,2},{2,1},{7,6},{6,5},{11,10},{10,9},{15,14},{14,13},{19,18},{18... | collective-permute-start | bytes 4718600 | tf_op jit(solution)/shard_map/ppermute | solution.py:48
  287.9 8.7 %slice-start.5 = ((s8[9437184]{0:T(1024)(128)(4,1)}), s8[4194304]{0:T(1024)(128)(4,1)S(1)}, s32[]{:S(2)}) async-start(s8[9437184]{0:T(1024)(128)(4,1)} %bitcast.124), calls=%async_computation.5 | async-start | bytes 8388608
  288.6 39.2 %collective-permute-start.15 = (bf16[128,6144]{1,0:T(8,128)(2,1)S(1)}, bf16[128,6144]{1,0:T(8,128)(2,1)S(1)}, u32[]{:S(2)}, u32[]{:S(2)}) collective-permute-start(bf16[128,6144]{1,0:T(8,128)(2,1)S(1)} %add_convert_fusion.1), channel_id=1, source_target_pairs={{3,2},{2,1},{1,0},{7,6},{6,5},{5,4},{11,10},{10,9},{9,8},{15,14},{... | collective-permute-start | bytes 4718600 | tf_op jit(solution)/shard_map/ppermute | solution.py:48
  290.0 38.9 %collective-permute-start.14 = (bf16[128,6144]{1,0:T(8,128)(2,1)S(1)}, bf16[128,6144]{1,0:T(8,128)(2,1)S(1)}, u32[]{:S(2)}, u32[]{:S(2)}) collective-permute-start(bf16[128,6144]{1,0:T(8,128)(2,1)S(1)} %add_convert_fusion.2), channel_id=1, source_target_pairs={{0,1},{1,2},{2,3},{4,5},{5,6},{6,7},{8,9},{9,10},{10,11},{12,13},{... | collective-permute-start | bytes 4718600 | tf_op jit(solution)/shard_map/ppermute | solution.py:45

commit v2 on v1

--- a/solution.py
+++ b/solution.py
@@ -1,30 +1,95 @@
+import functools
+
 import jax
 import jax.numpy as jnp
 from jax import lax
+from jax.experimental import pallas as pl
+from jax.experimental.pallas import tpu as pltpu
 from jax.sharding import PartitionSpec as P
 
 
-def head_layer_norm(raw_proj, gain):
-    local_heads = gain.shape[0]
-    head_size = gain.shape[1]
-    shaped = raw_proj.reshape(raw_proj.shape[0], local_heads, head_size)
-    head_mean = jnp.mean(shaped, axis=-1, keepdims=True)
-    centred = shaped - head_mean
-    head_var = jnp.mean(centred * centred, axis=-1, keepdims=True)
-    return (centred * lax.rsqrt(head_var + 1e-06) * gain[None, :, :]).astype(jnp.bfloat16)
+def project_kernel(head_size, x_ref, w_ref, qg_ref, kg_ref, q_ref, kv_ref):
+    shard = x_ref[...]
+    raw = [jnp.dot(shard, w_ref[c], preferred_element_type=jnp.float32) for c in range(3)]
+
+    def normal(part, gain):
+        centred = part - jnp.mean(part, axis=-1, keepdims=True)
+        var = jnp.mean(centred * centred, axis=-1, keepdims=True)
+        return (centred * lax.rsqrt(var + 1e-06) * gain).astype(jnp.bfloat16)
+
+    for start in range(0, q_ref.shape[1], head_size):
+        cols = slice(start, start + head_size)
+        q_ref[:, cols] = normal(raw[0][:, cols], qg_ref[:, cols])
+        kv_ref[0, :, cols] = normal(raw[1][:, cols], kg_ref[:, cols])
+    kv_ref[1] = raw[2].astype(jnp.bfloat16)
 
 
-def attend(queries, keys, values, scaling):
-    scores = (
-        jnp.einsum("qhd,khd->qhk", queries, keys, preferred_element_type=jnp.float32) * scaling
-    )
-    peak = jnp.max(scores, axis=-1, keepdims=True)
-    probs = jnp.exp(scores - peak)
-    total = jnp.sum(probs, axis=-1)
-    weighted = jnp.einsum(
-        "qhk,khd->qhd", probs.astype(jnp.bfloat16), values, preferred_element_type=jnp.float32
-    )
-    return (weighted / total[..., None]).astype(jnp.bfloat16)
+def project(shard, weight, query_gain, key_gain, head_size):
+    rows, depth = shard.shape
+    width = weight.shape[2]
+    block = 2 * head_size if width % (2 * head_size) == 0 else head_size
+    return pl.pallas_call(
+        functools.partial(project_kernel, head_size),
+        grid=(width // block,),
+        in_specs=[
+            pl.BlockSpec((rows, depth), lambda g: (0, 0)),
+            pl.BlockSpec((3, depth, block), lambda g: (0, 0, g)),
+            pl.BlockSpec((1, block), lambda g: (0, g)),
+            pl.BlockSpec((1, block), lambda g: (0, g)),
+        ],
+        out_specs=[
+            pl.BlockSpec((rows, block), lambda g: (0, g)),
+            pl.BlockSpec((2, rows, block), lambda g: (0, 0, g)),
+        ],
+        out_shape=[
+            jax.ShapeDtypeStruct((rows, width), jnp.bfloat16),
+            jax.ShapeDtypeStruct((2, rows, width), jnp.bfloat16),
+        ],
+        compiler_params=pltpu.CompilerParams(vmem_limit_bytes=40 << 20),
+        cost_estimate=pl.CostEstimate(
+            flops=6 * rows * depth * width, bytes_accessed=6 * depth * width, transcendentals=0
+        ),
+        name="project",
+    )(shard, weight, query_gain, key_gain)
+
+
+def attend_kernel(n_queries, scaling, *refs):
+    query_refs, kv_refs, out_ref = refs[:n_queries], refs[n_queries:-1], refs[-1]
+    keys = jnp.concatenate([ref[0] for ref in kv_refs], axis=0)
+    values = jnp.concatenate([ref[1] for ref in kv_refs], axis=0)
+    rows = query_refs[0].shape[0]
+    for number, ref in enumerate(query_refs):
+        scores = (
+            lax.dot_general(
+                ref[...], keys, (((1,), (1,)), ((), ())), preferred_element_type=jnp.float32
+            )
+            * scaling
+        )
+        probs = jnp.exp(scores - jnp.max(scores, axis=-1, keepdims=True))
+        total = jnp.sum(probs, axis=-1, keepdims=True)
+        mixed = jnp.dot(probs.astype(jnp.bfloat16), values, preferred_element_type=jnp.float32)
+        out_ref[number * rows : (number + 1) * rows, :] = (mixed / total).astype(jnp.bfloat16)
+
+
+def attend(queries, pieces, head_size, scaling):
+    rows, width = queries[0].shape
+    total = rows * len(queries)
+    keys = rows * len(pieces)
+    return pl.pallas_call(
+        functools.partial(attend_kernel, len(queries), scaling),
+        grid=(width // head_size,),
+        in_specs=[pl.BlockSpec((rows, head_size), lambda h: (0, h))] * len(queries)
+        + [pl.BlockSpec((2, rows, head_size), lambda h: (0, 0, h))] * len(pieces),
+        out_specs=pl.BlockSpec((total, head_size), lambda h: (0, h)),
+        out_shape=jax.ShapeDtypeStruct((total, width), jnp.bfloat16),
+        compiler_params=pltpu.CompilerParams(vmem_limit_bytes=40 << 20),
+        cost_estimate=pl.CostEstimate(
+            flops=4 * total * keys * width,
+            bytes_accessed=4 * (total + keys) * width,
+            transcendentals=total * keys * width // head_size,
+        ),
+        name="attend",
+    )(*queries, *pieces)
 
 
 def on_device(tokens, norm_gain, qkv_weight, query_gain, key_gain, out_weight):
@@ -60,7 +125,8 @@
     slots = [(normed, place)]
     for step in range(1, half + 1):
         if step < count:
-            slots.append((either(step), jnp.where(place >= step, place - step, place + step)))
+            shard, from_right[step] = lax.optimization_barrier((either(step), from_right[step]))
+            slots.append((shard, jnp.where(place >= step, place - step, place + step)))
     for extra in range(1, count - half):
         step, other = half + extra, half - extra
         far = longest >= step
@@ -75,30 +141,24 @@
             )
         )
 
-    queries = jnp.zeros((count * rows, local_heads, head_size), jnp.bfloat16)
-    keys, values = [], []
+    gains = query_gain.reshape(1, width), key_gain.reshape(1, width)
+    queries, pieces = [], []
     for shard, origin in slots:
-        raw = jnp.einsum("nd,cdk->cnk", shard, qkv_weight, preferred_element_type=jnp.float32)
-        queries = lax.dynamic_update_slice_in_dim(
-            queries, head_layer_norm(raw[0], query_gain), origin * rows, 0
-        )
-        key_now = head_layer_norm(raw[1], key_gain)
-        value_now = raw[2].astype(jnp.bfloat16)
-        both = jnp.concatenate([key_now.reshape(rows, width), value_now], axis=1)
-        held = [both]
+        query_now, both = project(shard, qkv_weight, *gains, head_size)
+        queries.append(query_now)
+        pieces.append(both)
         for turn in range(1, cores):
-            held.append(lax.ppermute(both, "seq", [(i, (i + turn) % cores) for i in range(cores)]))
-        for piece in held:
-            keys.append(piece[:, :width])
-            values.append(piece[:, width:])
-    keys_all = jnp.concatenate(keys, 0).reshape(-1, local_heads, head_size)
-    values_all = jnp.concatenate(values, 0).reshape(-1, local_heads, head_size)
-
-    attended = attend(queries, keys_all, values_all, scaling).reshape(count * rows, width)
+            pieces.append(
+                lax.ppermute(both, "seq", [(i, (i + turn) % cores) for i in range(cores)])
+            )
+    attended = attend(queries, pieces, head_size, scaling)
 
     def share(block):
-        piece = lax.dynamic_slice_in_dim(attended, block * rows, rows, 0)
-        return jnp.dot(piece, out_weight, preferred_element_type=jnp.float32)
+        slot = sum(number * (origin == block) for number, (_, origin) in enumerate(slots))
+        piece = lax.dynamic_slice_in_dim(attended, slot * rows, rows, 0)
+        return lax.optimization_barrier(
+            jnp.dot(piece, out_weight, preferred_element_type=jnp.float32)
+        )
 
     got_left = got_right = None
     for step in range(1, count):

time: 332 us -> 290 us (0.87)
  matrix products: 71.7 us -> 16.8 us
  Pallas kernels: 0 us -> 54.5 us
  local copies, waits for them, and re-layouts: 52.3 us -> 8.9 us
  waiting for transfers between devices: 137 us -> 156 us
  other arithmetic: 35.7 us -> 16.9 us
    dot_general x10 -> x4, matrix products: 71.7 us -> 16.8 us  [share(): jnp.dot(piece, out_weight, preferred_element_type=jnp.float32)]
    pallas_call x0 -> x5, Pallas kernels: none -> 54.5 us  [the longest x4 43.9 us: project(): pl.pallas_call(functools.partial(project_kernel, head_size), grid=(width...]
    slice x20 -> x0, local copies, waits for them, and re-layouts: 19.3 us -> none  [the longest x8 8.96 us: on_device(): raw[0]]
    ppermute x6, waiting for transfers between devices: 55.3 us -> 70.1 us  [leftward(): lax.ppermute(value, 'stream', [(i, i - 1) for i in range(first, last, -1)])]
    reduce_sum x17 -> x0, other arithmetic: 14 us -> none  [the longest x8 5.98 us: head_layer_norm(): head_var = jnp.mean(centred * centred, axis=-1, keepdims=True)]
    sub x8 -> x0, local copies, waits for them, and re-layouts: 7.3 us -> none  [head_layer_norm(): centred = shaped - head_mean]
    mul x8 -> x0, local copies, waits for them, and re-layouts: 7.29 us -> none  [head_layer_norm(): centred * lax.rsqrt(head_var + 1e-06) * gain[None, :, :]]
    convert_element_type x2 -> x0, other arithmetic: 5.26 us -> none  [head_layer_norm(): (centred * lax.rsqrt(head_var + 1e-06) * gain[None, :, :]).astype(jnp.bfl...]
  transfers between devices with their start and end apart: 16 -> 16, of which waited for: 8 -> 8; matrix products, arithmetic and copies ran while one was open for 25% -> 4% of each run, Pallas kernels for 0% -> 15%
where the time goes in v2:
time: 290 us
  waiting for transfers between devices  156 us (54%)
  Pallas kernels  54.5 us (19%)
  starting transfers between devices  36.5 us (13%)
  other arithmetic  16.9 us (6%)
  matrix products  16.8 us (6%)
  local copies, waits for them, and re-layouts  8.9 us (3%)
    ppermute x6, waiting for transfers between devices, rightward(): lax.ppermute(value, 'stream', [(i, i + 1) for i in range(first, last)])  83.8 us
    ppermute x6, waiting for transfers between devices, leftward(): lax.ppermute(value, 'stream', [(i, i - 1) for i in range(first, last, -1)])  70.1 us
    pallas_call x4, Pallas kernels, project(): pl.pallas_call(functools.partial(project_kernel, head_size), grid=(width...  43.9 us
    ppermute x6, starting transfers between devices, rightward(): lax.ppermute(value, 'stream', [(i, i + 1) for i in range(first, last)])  28.7 us
    dot_general x4, matrix products, share(): jnp.dot(piece, out_weight, preferred_element_type=jnp.float32)  16.8 us
    pallas_call x1, Pallas kernels, attend(): pl.pallas_call(functools.partial(attend_kernel, len(queries), scaling), g...  10.6 us
    unnamed x42, local copies, waits for them, and re-layouts  8.89 us
    ppermute x6, starting transfers between devices, leftward(): lax.ppermute(value, 'stream', [(i, i - 1) for i in range(first, last, -1)])  7.77 us
  transfers between devices with their start and end apart: 16, of which 8 were waited for; matrix products, arithmetic and copies ran while one was open for 4% of the time, Pallas kernels for 15%

profile of v2, /device:TPU:0, one launch (start us, length us, event | category | flops | bytes accessed | tf_op | source)
XLA Modules:
  0.0 289.7 jit_solution(8337923223951196691)
XLA Ops:
  0.0 1.8 convert_reduce_fusion
  1.8 2.0 fusion.2
  3.8 0.6 fusion.4.x_ref
  4.4 1.3 collective-permute-start.1
  5.7 6.7 %collective-permute-start = (bf16[128,6144]{1,0:T(8,128)(2,1)S(1)}, bf16[128,6144]{1,0:T(8,128)(2,1)}, u32[]{:S(2)}, u32[]{:S(2)}) collective-permute-start(bf16[128,6144]{1,0:T(8,128)(2,1)S(1)} %fusion.4.x_ref), channel_id=1, source_target_pairs={{0,1},{1,2},{2,3},{4,5},{5,6},{6,7},{8,9},{9,10},{10,11},{12,13},{... | collective-permute-start | bytes 4718600 | tf_op jit(solution)/shard_map/ppermute | solution.py:110
  12.5 11.0 %project.4 = (bf16[128,768]{1,0:T(8,128)(2,1)S(1)}, bf16[2,128,768]{2,1,0:T(8,128)(2,1)S(1)}) custom-call(bf16[128,6144]{1,0:T(8,128)(2,1)S(1)} %fusion.4.x_ref, bf16[3,6144,768]{2,1,0:T(8,128)(2,1)} %w_ref.7, f32[1,768]{1,0:T(1,128)S(1)} %get-tuple-element.42.qg_ref, f32[1,768]{1,0:T(1,128)S(1)} %get-tuple-element.41.kg_ref), custom_call_target="tpu_custom_call" | custom-call | flops 3623878656 | bytes 28311552 | tf_op jit(solution)/shard_map/project/pallas_call | solution.py:31
  23.5 0.7 copy-done.2
  24.1 0.0 collective-permute-start.6
  24.1 19.7 %collective-permute-done.1 = bf16[128,6144]{1,0:T(8,128)(2,1)} collective-permute-done((bf16[128,6144]{1,0:T(8,128)(2,1)S(1)}, bf16[128,6144]{1,0:T(8,128)(2,1)}, u32[]{:S(2)}, u32[]{:S(2)}) %collective-permute-start.1) | collective-permute-done | bytes 1572896 | tf_op jit(solution)/shard_map/ppermute | solution.py:113
  43.9 1.3 collective-permute-start.3
  45.1 0.0 collective-permute-done
  45.2 0.8 collective-permute-start.2
  45.9 1.6 broadcast_select_fusion.1.x_ref
  47.5 11.0 %project.5 = (bf16[128,768]{1,0:T(8,128)(2,1)S(1)}, bf16[2,128,768]{2,1,0:T(8,128)(2,1)S(1)}) custom-call(bf16[128,6144]{1,0:T(8,128)(2,1)S(1)} %broadcast_select_fusion.1.x_ref, bf16[3,6144,768]{2,1,0:T(8,128)(2,1)} %w_ref.7, f32[1,768]{1,0:T(1,128)S(1)} %get-tuple-element.42.qg_ref, f32[1,768]{1,0:T(1,128)S(1)} %get-tuple-element.41.kg_ref), custom_call_target="tpu_custom_call" | custom-call | flops 3623878656 | bytes 28311552 | tf_op jit(solution)/shard_map/project/pallas_call | solution.py:31
  58.5 0.7 copy-done.4
  59.2 0.0 collective-permute-start.7
  59.2 22.3 %collective-permute-done.3 = bf16[128,6144]{1,0:T(8,128)(2,1)S(1)} collective-permute-done((bf16[128,6144]{1,0:T(8,128)(2,1)}, bf16[128,6144]{1,0:T(8,128)(2,1)S(1)}, u32[]{:S(2)}, u32[]{:S(2)}) %collective-permute-start.3) | collective-permute-done | bytes 1572896 | tf_op jit(solution)/shard_map/ppermute | solution.py:113
  81.5 1.3 collective-permute-start.5
  82.8 0.0 collective-permute-done.2
  82.8 0.9 collective-permute-start.4
  83.8 0.2 broadcast_select_fusion.x_ref
  83.9 11.0 %project.6 = (bf16[128,768]{1,0:T(8,128)(2,1)S(1)}, bf16[2,128,768]{2,1,0:T(8,128)(2,1)S(1)}) custom-call(bf16[128,6144]{1,0:T(8,128)(2,1)S(1)} %broadcast_select_fusion.x_ref, bf16[3,6144,768]{2,1,0:T(8,128)(2,1)} %w_ref.7, f32[1,768]{1,0:T(1,128)S(1)} %get-tuple-element.42.qg_ref, f32[1,768]{1,0:T(1,128)S(1)} %get-tuple-element.41.kg_ref), custom_call_target="tpu_custom_call" | custom-call | flops 3623878656 | bytes 28311552 | tf_op jit(solution)/shard_map/project/pallas_call | solution.py:31
  94.9 0.7 copy-done.6
  95.6 0.0 collective-permute-start.8
  95.6 22.5 %collective-permute-done.5 = bf16[128,6144]{1,0:T(8,128)(2,1)S(1)} collective-permute-done((bf16[128,6144]{1,0:T(8,128)(2,1)S(1)}, bf16[128,6144]{1,0:T(8,128)(2,1)S(1)}, u32[]{:S(2)}, u32[]{:S(2)}) %collective-permute-start.5) | collective-permute-done | bytes 1572896 | tf_op jit(solution)/shard_map/ppermute | solution.py:113
  118.1 0.0 collective-permute-done.4
  118.1 0.2 select_select_fusion.x_ref
  118.3 11.0 %project.7 = (bf16[128,768]{1,0:T(8,128)(2,1)S(1)}, bf16[2,128,768]{2,1,0:T(8,128)(2,1)S(1)}) custom-call(bf16[128,6144]{1,0:T(8,128)(2,1)S(1)} %select_select_fusion.x_ref, bf16[3,6144,768]{2,1,0:T(8,128)(2,1)} %w_ref.7, f32[1,768]{1,0:T(1,128)S(1)} %get-tuple-element.42.qg_ref, f32[1,768]{1,0:T(1,128)S(1)} %get-tuple-element.41.kg_ref), custom_call_target="tpu_custom_call" | custom-call | flops 3623878656 | bytes 28311552 | tf_op jit(solution)/shard_map/project/pallas_call | solution.py:31
  129.3 0.7 copy-done.8
  130.0 0.0 collective-permute-start.9
  130.0 0.0 collective-permute-done.8.refs_9_
  130.0 1.7 collective-permute-done.9.refs_11_
  131.7 0.7 copy-done
  132.5 1.0 copy-done.1
  133.4 0.9 copy-done.3
  134.4 0.9 copy-done.5
  135.3 0.9 copy-done.7
  136.2 0.9 copy-done.9
  137.2 10.6 %attend.1 = bf16[512,768]{1,0:T(8,128)(2,1)S(1)} custom-call(bf16[128,768]{1,0:T(8,128)(2,1)S(1)} %copy-done.3, bf16[128,768]{1,0:T(8,128)(2,1)S(1)} %copy-done.5, bf16[128,768]{1,0:T(8,128)(2,1)S(1)} %copy-done.7, bf16[128,768]{1,0:T(8,128)(2,1)S(1)} %copy-done.9, bf16[2,128,768]{2,1,0:T(8,128)(2,1)S(1)} %get-tuple-element.29.refs_4_, ...), custom_call_target="tpu_custom_call" | custom-call | flops 1610612736 | bytes 4718592 | tf_op jit(solution)/shard_map/attend/pallas_call | solution.py:78
  147.7 0.0 slice-start.1
  147.8 0.0 slice-start.2
  147.8 5.2 %fusion.5 = f32[128,6144]{1,0:T(8,128)S(1)} fusion(bf16[768,6144]{1,0:T(8,128)(2,1)} %param.11, bf16[512,768]{1,0:T(8,128)(2,1)S(1)} %attend.1, s32[]{:T(128)S(6)} %select_n.69), kind=kOutput, calls=%fused_computation.15 | convolution fusion | flops 1207959552 | bytes 12779524 | tf_op jit(solution)/shard_map/dot_general | solution.py:160
  153.0 1.5 convert_element_type.80
  154.5 1.4 fusion.9
  155.9 1.5 convert_element_type.81
  157.4 0.7 copy-done.12
  158.1 2.9 %collective-permute-start.10 = (bf16[128,6144]{1,0:T(8,128)(2,1)}, bf16[128,6144]{1,0:T(8,128)(2,1)S(1)}, u32[]{:S(2)}, u32[]{:S(2)}) collective-permute-start(bf16[128,6144]{1,0:T(8,128)(2,1)} %convert_element_type.80), channel_id=1, source_target_pairs={{0,1},{4,5},{8,9},{12,13},{16,17},{20,21},{24,25},{28,29}} | collective-permute-start | bytes 4718600 | tf_op jit(solution)/shard_map/ppermute | solution.py:110
  161.1 1.9 collective-permute-start.11
  163.0 5.1 %fusion.7 = f32[128,6144]{1,0:T(8,128)S(1)} fusion(bf16[768,6144]{1,0:T(8,128)(2,1)} %param.11, bf16[512,768]{1,0:T(8,128)(2,1)S(1)} %attend.1, s32[]{:T(128)S(6)} %select_n.68), kind=kOutput, calls=%fused_computation.17 | convolution fusion | flops 1207959552 | bytes 12779524 | tf_op jit(solution)/shard_map/dot_general | solution.py:160
  168.0 27.2 %collective-permute-done.10 = bf16[128,6144]{1,0:T(8,128)(2,1)S(1)} collective-permute-done((bf16[128,6144]{1,0:T(8,128)(2,1)}, bf16[128,6144]{1,0:T(8,128)(2,1)S(1)}, u32[]{:S(2)}, u32[]{:S(2)}) %collective-permute-start.10) | collective-permute-done | bytes 1572896 | tf_op jit(solution)/shard_map/ppermute | solution.py:110
  195.2 0.0 collective-permute-done.11
  195.2 2.2 add_convert_fusion.3
  197.5 4.6 %collective-permute-start.12 = (bf16[128,6144]{1,0:T(8,128)(2,1)S(1)}, bf16[128,6144]{1,0:T(8,128)(2,1)S(1)}, u32[]{:S(2)}, u32[]{:S(2)}) collective-permute-start(bf16[128,6144]{1,0:T(8,128)(2,1)S(1)} %get-tuple-element.35), channel_id=1, source_target_pairs={{0,1},{1,2},{4,5},{5,6},{8,9},{9,10},{12,13},{13,14},{16,17},{17,1... | collective-permute-start | bytes 4718600 | tf_op jit(solution)/shard_map/ppermute | solution.py:110
  202.1 0.8 collective-permute-start.13
  202.9 32.2 %collective-permute-done.12 = bf16[128,6144]{1,0:T(8,128)(2,1)S(1)} collective-permute-done((bf16[128,6144]{1,0:T(8,128)(2,1)S(1)}, bf16[128,6144]{1,0:T(8,128)(2,1)S(1)}, u32[]{:S(2)}, u32[]{:S(2)}) %collective-permute-start.12) | collective-permute-done | bytes 1572896 | tf_op jit(solution)/shard_map/ppermute | solution.py:110
  235.1 0.3 add_convert_fusion.2
  235.4 0.0 collective-permute-done.13
  235.4 1.6 add_convert_fusion.1
  237.0 12.7 %collective-permute-start.14 = (bf16[128,6144]{1,0:T(8,128)(2,1)S(1)}, bf16[128,6144]{1,0:T(8,128)(2,1)}, u32[]{:S(2)}, u32[]{:S(2)}) collective-permute-start(bf16[128,6144]{1,0:T(8,128)(2,1)S(1)} %add_convert_fusion.2), channel_id=1, source_target_pairs={{0,1},{1,2},{2,3},{4,5},{5,6},{6,7},{8,9},{9,10},{10,11},{12,13},{... | collective-permute-start | bytes 4718600 | tf_op jit(solution)/shard_map/ppermute | solution.py:110
  249.7 1.3 collective-permute-start.15
  251.0 5.1 %fusion.11 = f32[128,6144]{1,0:T(8,128)S(1)} fusion(bf16[768,6144]{1,0:T(8,128)(2,1)} %param.11, bf16[512,768]{1,0:T(8,128)(2,1)S(1)} %attend.1, s32[]{:T(128)S(6)} %select_n.66), kind=kOutput, calls=%fused_computation.21 | convolution fusion | flops 1207959552 | bytes 12779524 | tf_op jit(solution)/shard_map/dot_general | solution.py:160
  256.1 24.4 %collective-permute-done.14 = bf16[128,6144]{1,0:T(8,128)(2,1)} collective-permute-done((bf16[128,6144]{1,0:T(8,128)(2,1)S(1)}, bf16[128,6144]{1,0:T(8,128)(2,1)}, u32[]{:S(2)}, u32[]{:S(2)}) %collective-permute-start.14) | collective-permute-done | bytes 1572896 | tf_op jit(solution)/shard_map/ppermute | solution.py:110
  280.5 5.6 %collective-permute-done.15 = bf16[128,6144]{1,0:T(8,128)(2,1)} collective-permute-done((bf16[128,6144]{1,0:T(8,128)(2,1)}, bf16[128,6144]{1,0:T(8,128)(2,1)}, u32[]{:S(2)}, u32[]{:S(2)}) %collective-permute-start.15) | collective-permute-done | bytes 1572896 | tf_op jit(solution)/shard_map/ppermute | solution.py:113
  286.1 3.6 %add_convert_fusion = bf16[128,6144]{1,0:T(8,128)(2,1)} fusion(bf16[128,6144]{1,0:T(8,128)(2,1)} %collective-permute-done.15, f32[128,6144]{1,0:T(8,128)S(1)} %fusion.11, bf16[128,6144]{1,0:T(8,128)(2,1)} %collective-permute-done.14), kind=kLoop, calls=%fused_computation.7 | loop fusion | flops 3932160 | bytes 7864320 | tf_op jit(solution)/shard_map/convert_element_type | solution.py:178
  (35 shorter events, 0.1 us)
Async XLA Ops:
  0.0 3.8 %copy-start.14 = (bf16[128,6144]{1,0:T(8,128)(2,1)S(1)}, bf16[128,6144]{1,0:T(8,128)(2,1)}, u32[]{:S(2)}) copy-start(bf16[128,6144]{1,0:T(8,128)(2,1)} %param.6) | copy-start | bytes 4718596
  0.0 3.8 %copy-start.15 = (f32[6144]{0:T(1024)S(1)}, f32[6144]{0:T(1024)}, u32[]{:S(2)}) copy-start(f32[6144]{0:T(1024)} %param.7) | copy-start | bytes 73732
  0.0 12.4 %copy-start.16 = (f32[6,128]{1,0:T(8,128)S(1)}, f32[6,128]{1,0:T(8,128)}, u32[]{:S(2)}) copy-start(f32[6,128]{1,0:T(8,128)} %param.10) | copy-start | bytes 9220
  0.0 12.4 %copy-start.17 = (f32[6,128]{1,0:T(8,128)S(1)}, f32[6,128]{1,0:T(8,128)}, u32[]{:S(2)}) copy-start(f32[6,128]{1,0:T(8,128)} %param.9) | copy-start | bytes 9220
  4.4 39.5 %collective-permute-start.1 = (bf16[128,6144]{1,0:T(8,128)(2,1)S(1)}, bf16[128,6144]{1,0:T(8,128)(2,1)}, u32[]{:S(2)}, u32[]{:S(2)}) collective-permute-start(bf16[128,6144]{1,0:T(8,128)(2,1)S(1)} %fusion.4.x_ref), channel_id=1, source_target_pairs={{3,2},{2,1},{1,0},{7,6},{6,5},{5,4},{11,10},{10,9},{9,8},{15,14},{... | collective-permute-start | bytes 4718600 | tf_op jit(solution)/shard_map/ppermute | solution.py:113
  5.7 39.5 %collective-permute-start = (bf16[128,6144]{1,0:T(8,128)(2,1)S(1)}, bf16[128,6144]{1,0:T(8,128)(2,1)}, u32[]{:S(2)}, u32[]{:S(2)}) collective-permute-start(bf16[128,6144]{1,0:T(8,128)(2,1)S(1)} %fusion.4.x_ref), channel_id=1, source_target_pairs={{0,1},{1,2},{2,3},{4,5},{5,6},{6,7},{8,9},{9,10},{10,11},{12,13},{... | collective-permute-start | bytes 4718600 | tf_op jit(solution)/shard_map/ppermute | solution.py:110
  23.4 0.7 copy-start.2
  24.1 105.9 %collective-permute-start.6 = (bf16[2,128,768]{2,1,0:T(8,128)(2,1)S(1)}, bf16[2,128,768]{2,1,0:T(8,128)(2,1)S(1)}, u32[]{:S(2)}, u32[]{:S(2)}) collective-permute-start(bf16[2,128,768]{2,1,0:T(8,128)(2,1)S(1)} %get-tuple-element.29.refs_4_), channel_id=1, source_target_pairs={{0,4},{4,0},{1,5},{5,1},{2,6},{6,2},{3,7},{7,3},{8,12},{12,8},{9,1... | collective-permute-start | bytes 1179656 | tf_op jit(solution)/shard_map/ppermute | solution.py:152
  43.9 37.7 %collective-permute-start.3 = (bf16[128,6144]{1,0:T(8,128)(2,1)}, bf16[128,6144]{1,0:T(8,128)(2,1)S(1)}, u32[]{:S(2)}, u32[]{:S(2)}) collective-permute-start(bf16[128,6144]{1,0:T(8,128)(2,1)} %collective-permute-done.1), channel_id=1, source_target_pairs={{2,1},{1,0},{6,5},{5,4},{10,9},{9,8},{14,13},{13,12},{18,17},{17,1... | collective-permute-start | bytes 4718600 | tf_op jit(solution)/shard_map/ppermute | solution.py:113
  45.2 37.6 %collective-permute-start.2 = (bf16[128,6144]{1,0:T(8,128)(2,1)}, bf16[128,6144]{1,0:T(8,128)(2,1)S(1)}, u32[]{:S(2)}, u32[]{:S(2)}) collective-permute-start(bf16[128,6144]{1,0:T(8,128)(2,1)} %collective-permute-done), channel_id=1, source_target_pairs={{1,2},{2,3},{5,6},{6,7},{9,10},{10,11},{13,14},{14,15},{17,18},{18... | collective-permute-start | bytes 4718600 | tf_op jit(solution)/shard_map/ppermute | solution.py:110
  58.5 0.7 copy-start.4
  59.2 70.8 %collective-permute-start.7 = (bf16[2,128,768]{2,1,0:T(8,128)(2,1)S(1)}, bf16[2,128,768]{2,1,0:T(8,128)(2,1)S(1)}, u32[]{:S(2)}, u32[]{:S(2)}) collective-permute-start(bf16[2,128,768]{2,1,0:T(8,128)(2,1)S(1)} %get-tuple-element.30.refs_6_), channel_id=1, source_target_pairs={{0,4},{4,0},{1,5},{5,1},{2,6},{6,2},{3,7},{7,3},{8,12},{12,8},{9,1... | collective-permute-start | bytes 1179656 | tf_op jit(solution)/shard_map/ppermute | solution.py:152
  81.5 36.6 %collective-permute-start.5 = (bf16[128,6144]{1,0:T(8,128)(2,1)S(1)}, bf16[128,6144]{1,0:T(8,128)(2,1)S(1)}, u32[]{:S(2)}, u32[]{:S(2)}) collective-permute-start(bf16[128,6144]{1,0:T(8,128)(2,1)S(1)} %collective-permute-done.3), channel_id=1, source_target_pairs={{1,0},{5,4},{9,8},{13,12},{17,16},{21,20},{25,24},{29,28}} | collective-permute-start | bytes 4718600 | tf_op jit(solution)/shard_map/ppermute | solution.py:113
  82.8 35.3 %collective-permute-start.4 = (bf16[128,6144]{1,0:T(8,128)(2,1)S(1)}, bf16[128,6144]{1,0:T(8,128)(2,1)S(1)}, u32[]{:S(2)}, u32[]{:S(2)}) collective-permute-start(bf16[128,6144]{1,0:T(8,128)(2,1)S(1)} %collective-permute-done.2), channel_id=1, source_target_pairs={{2,3},{6,7},{10,11},{14,15},{18,19},{22,23},{26,27},{30,31}} | collective-permute-start | bytes 4718600 | tf_op jit(solution)/shard_map/ppermute | solution.py:110
  94.9 0.7 copy-start.6
  95.6 34.4 %collective-permute-start.8 = (bf16[2,128,768]{2,1,0:T(8,128)(2,1)S(1)}, bf16[2,128,768]{2,1,0:T(8,128)(2,1)S(1)}, u32[]{:S(2)}, u32[]{:S(2)}) collective-permute-start(bf16[2,128,768]{2,1,0:T(8,128)(2,1)S(1)} %get-tuple-element.31.refs_8_), channel_id=1, source_target_pairs={{0,4},{4,0},{1,5},{5,1},{2,6},{6,2},{3,7},{7,3},{8,12},{12,8},{9,1... | collective-permute-start | bytes 1179656 | tf_op jit(solution)/shard_map/ppermute | solution.py:152
  129.3 0.7 copy-start.8
  130.0 1.7 collective-permute-start.9
  131.7 0.7 copy-start
  132.4 1.0 copy-start.1
  133.4 0.9 copy-start.3
  134.4 0.9 copy-start.5
  135.3 0.9 copy-start.7
  136.2 0.9 copy-start.9
  137.2 17.4 %slice-start = ((s8[9437184]{0:T(1024)(128)(4,1)}), s8[1048576]{0:T(1024)(128)(4,1)S(1)}, s32[]{:S(2)}) async-start(s8[9437184]{0:T(1024)(128)(4,1)} %bitcast.12), calls=%async_computation | async-start | bytes 2097152
  147.7 6.8 %slice-start.1 = ((s8[9437184]{0:T(1024)(128)(4,1)}), s8[4194304]{0:T(1024)(128)(4,1)S(1)}, s32[]{:S(2)}) async-start(s8[9437184]{0:T(1024)(128)(4,1)} %bitcast.12), calls=%async_computation.1 | async-start | bytes 8388608
  147.8 6.8 %slice-start.2 = ((s8[9437184]{0:T(1024)(128)(4,1)}), s8[4194304]{0:T(1024)(128)(4,1)S(1)}, s32[]{:S(2)}) async-start(s8[9437184]{0:T(1024)(128)(4,1)} %bitcast.12), calls=%async_computation.2 | async-start | bytes 8388608
  153.0 2.9 %copy-start.10 = (f32[128,6144]{1,0:T(8,128)}, f32[128,6144]{1,0:T(8,128)S(1)}, u32[]{:S(2)}) copy-start(f32[128,6144]{1,0:T(8,128)S(1)} %fusion.5) | copy-start | bytes 9437188
  155.9 2.2 copy-start.12
  158.1 37.1 %collective-permute-start.10 = (bf16[128,6144]{1,0:T(8,128)(2,1)}, bf16[128,6144]{1,0:T(8,128)(2,1)S(1)}, u32[]{:S(2)}, u32[]{:S(2)}) collective-permute-start(bf16[128,6144]{1,0:T(8,128)(2,1)} %convert_element_type.80), channel_id=1, source_target_pairs={{0,1},{4,5},{8,9},{12,13},{16,17},{20,21},{24,25},{28,29}} | collective-permute-start | bytes 4718600 | tf_op jit(solution)/shard_map/ppermute | solution.py:110
  161.1 34.2 %collective-permute-start.11 = (bf16[128,6144]{1,0:T(8,128)(2,1)}, bf16[128,6144]{1,0:T(8,128)(2,1)}, u32[]{:S(2)}, u32[]{:S(2)}) collective-permute-start(bf16[128,6144]{1,0:T(8,128)(2,1)} %convert_element_type.81), channel_id=1, source_target_pairs={{3,2},{7,6},{11,10},{15,14},{19,18},{23,22},{27,26},{31,30}} | collective-permute-start | bytes 4718600 | tf_op jit(solution)/shard_map/ppermute | solution.py:113
  168.0 67.1 %copy-start.13 = (f32[128,6144]{1,0:T(8,128)S(1)}, f32[128,6144]{1,0:T(8,128)}, u32[]{:S(2)}) copy-start(f32[128,6144]{1,0:T(8,128)} %copy-done.12) | copy-start | bytes 9437188
  197.5 38.0 %copy-start.11 = (f32[128,6144]{1,0:T(8,128)S(1)}, f32[128,6144]{1,0:T(8,128)}, u32[]{:S(2)}) copy-start(f32[128,6144]{1,0:T(8,128)} %copy-done.10) | copy-start | bytes 9437188
  197.5 37.6 %collective-permute-start.12 = (bf16[128,6144]{1,0:T(8,128)(2,1)S(1)}, bf16[128,6144]{1,0:T(8,128)(2,1)S(1)}, u32[]{:S(2)}, u32[]{:S(2)}) collective-permute-start(bf16[128,6144]{1,0:T(8,128)(2,1)S(1)} %get-tuple-element.35), channel_id=1, source_target_pairs={{0,1},{1,2},{4,5},{5,6},{8,9},{9,10},{12,13},{13,14},{16,17},{17,1... | collective-permute-start | bytes 4718600 | tf_op jit(solution)/shard_map/ppermute | solution.py:110
  202.1 33.3 %collective-permute-start.13 = (bf16[128,6144]{1,0:T(8,128)(2,1)S(1)}, bf16[128,6144]{1,0:T(8,128)(2,1)S(1)}, u32[]{:S(2)}, u32[]{:S(2)}) collective-permute-start(bf16[128,6144]{1,0:T(8,128)(2,1)S(1)} %get-tuple-element.36), channel_id=1, source_target_pairs={{3,2},{2,1},{7,6},{6,5},{11,10},{10,9},{15,14},{14,13},{19,18},{18... | collective-permute-start | bytes 4718600 | tf_op jit(solution)/shard_map/ppermute | solution.py:113
  237.0 43.5 %collective-permute-start.14 = (bf16[128,6144]{1,0:T(8,128)(2,1)S(1)}, bf16[128,6144]{1,0:T(8,128)(2,1)}, u32[]{:S(2)}, u32[]{:S(2)}) collective-permute-start(bf16[128,6144]{1,0:T(8,128)(2,1)S(1)} %add_convert_fusion.2), channel_id=1, source_target_pairs={{0,1},{1,2},{2,3},{4,5},{5,6},{6,7},{8,9},{9,10},{10,11},{12,13},{... | collective-permute-start | bytes 4718600 | tf_op jit(solution)/shard_map/ppermute | solution.py:110
  249.7 36.4 %collective-permute-start.15 = (bf16[128,6144]{1,0:T(8,128)(2,1)}, bf16[128,6144]{1,0:T(8,128)(2,1)}, u32[]{:S(2)}, u32[]{:S(2)}) collective-permute-start(bf16[128,6144]{1,0:T(8,128)(2,1)} %add_convert_fusion.1), channel_id=1, source_target_pairs={{3,2},{2,1},{1,0},{7,6},{6,5},{5,4},{11,10},{10,9},{9,8},{15,14},{... | collective-permute-start | bytes 4718600 | tf_op jit(solution)/shard_map/ppermute | solution.py:113

commit v3 on v2

--- a/solution.py
+++ b/solution.py
@@ -82,7 +82,7 @@
         + [pl.BlockSpec((2, rows, head_size), lambda h: (0, 0, h))] * len(pieces),
         out_specs=pl.BlockSpec((total, head_size), lambda h: (0, h)),
         out_shape=jax.ShapeDtypeStruct((total, width), jnp.bfloat16),
-        compiler_params=pltpu.CompilerParams(vmem_limit_bytes=40 << 20),
+        compiler_params=pltpu.CompilerParams(vmem_limit_bytes=60 << 20),
         cost_estimate=pl.CostEstimate(
             flops=4 * total * keys * width,
             bytes_accessed=4 * (total + keys) * width,
@@ -156,23 +156,29 @@
     def share(block):
         slot = sum(number * (origin == block) for number, (_, origin) in enumerate(slots))
         piece = lax.dynamic_slice_in_dim(attended, slot * rows, rows, 0)
-        return lax.optimization_barrier(
-            jnp.dot(piece, out_weight, preferred_element_type=jnp.float32)
-        )
+        return jnp.dot(piece, out_weight, preferred_element_type=jnp.float32)
 
     got_left = got_right = None
     for step in range(1, count):
-        right_sum = share(lax.rem(place - step + count, count))
-        left_sum = share(lax.rem(place + step, count))
-        if got_left is not None:
-            right_sum = right_sum + got_left
-            left_sum = left_sum + got_right
-        right_sum, left_sum = lax.optimization_barrier(
-            (right_sum.astype(jnp.bfloat16), left_sum.astype(jnp.bfloat16))
-        )
+        right_block = lax.rem(place - step + count, count)
+        left_block = lax.rem(place + step, count)
+        if 2 * step <= count:
+            block = jnp.where(place < step, right_block, left_block)
+            right_sum = share(block)
+            if got_left is not None:
+                right_sum = lax.optimization_barrier(right_sum) + got_left + got_right
+            left_sum = right_sum = right_sum.astype(jnp.bfloat16)
+        else:
+            right_sum = lax.optimization_barrier(share(right_block))
+            left_sum = lax.optimization_barrier(share(left_block))
+            if got_left is not None:
+                right_sum, left_sum = right_sum + got_left, left_sum + got_right
+            right_sum, left_sum = lax.optimization_barrier(
+                (right_sum.astype(jnp.bfloat16), left_sum.astype(jnp.bfloat16))
+            )
         got_left = rightward(right_sum, 0, step)
         got_right = leftward(left_sum, count - 1, count - 1 - step)
-    result = share(place)
+    result = lax.optimization_barrier(share(place))
     if got_left is not None:
         result = result + got_left + got_right
     return result.astype(jnp.bfloat16)

time: 290 us -> 283 us (0.976)
  matrix products: 16.8 us -> 23.3 us
  local copies, waits for them, and re-layouts: 8.9 us -> 3.49 us
  starting transfers between devices: 36.5 us -> 31.3 us
  waiting for transfers between devices: 156 us -> 153 us
    dot_general x4 -> x5, matrix products: 16.8 us -> 23.3 us  [share(): return jnp.dot(piece, out_weight, preferred_element_type=jnp.float32)]
    unnamed x42 -> x38, local copies, waits for them, and re-layouts: 8.89 us -> 3.49 us
    ppermute x6, starting transfers between devices: 28.7 us -> 24.6 us  [rightward(): lax.ppermute(value, 'stream', [(i, i + 1) for i in range(first, last)])]
    convert_element_type x3 -> x1, other arithmetic: 5.26 us -> 1.55 us  [on_device(): left_sum.astype(jnp.bfloat16)]
    convert_element_type x0 -> x1, other arithmetic: none -> 3.19 us  [on_device(): left_sum = right_sum = right_sum.astype(jnp.bfloat16)]
  transfers between devices with their start and end apart: 16 -> 16, of which waited for: 8 -> 8; matrix products, arithmetic and copies ran while one was open for 4% -> 8% of each run, Pallas kernels for 15% -> 16%
where the time goes in v3:
time: 283 us; the launch traced here: 282 us
  waiting for transfers between devices  153 us (54%)
  Pallas kernels  55.8 us (20%)
  starting transfers between devices  31.3 us (11%)
  matrix products  23.3 us (8%)
  other arithmetic  14.5 us (5%)
  local copies, waits for them, and re-layouts  3.49 us (1%)
    ppermute x6, waiting for transfers between devices, rightward(): lax.ppermute(value, 'stream', [(i, i + 1) for i in range(first, last)])  82.3 us
    ppermute x6, waiting for transfers between devices, leftward(): lax.ppermute(value, 'stream', [(i, i - 1) for i in range(first, last, -1)])  69.5 us
    pallas_call x4, Pallas kernels, project(): pl.pallas_call(functools.partial(project_kernel, head_size), grid=(width...  44 us
    ppermute x6, starting transfers between devices, rightward(): lax.ppermute(value, 'stream', [(i, i + 1) for i in range(first, last)])  24.6 us
    dot_general x5, matrix products, share(): return jnp.dot(piece, out_weight, preferred_element_type=jnp.float32)  23.3 us
    pallas_call x1, Pallas kernels, attend(): pl.pallas_call(functools.partial(attend_kernel, len(queries), scaling), g...  11.8 us
    ppermute x6, starting transfers between devices, leftward(): lax.ppermute(value, 'stream', [(i, i - 1) for i in range(first, last, -1)])  6.66 us
  transfers between devices with their start and end apart: 16, of which 8 were waited for; matrix products, arithmetic and copies ran while one was open for 8% of the time, Pallas kernels for 16%

profile of v3, /device:TPU:0, one launch (start us, length us, event | category | flops | bytes accessed | tf_op | source)
XLA Modules:
  0.0 282.1 jit_solution(987266626658372819)
XLA Ops:
  0.0 1.8 convert_reduce_fusion
  1.8 2.0 fusion.2
  3.8 0.0 copy-done.8
  3.8 0.0 copy-done.9
  3.8 0.6 fusion.4.x_ref
  4.4 1.3 collective-permute-start.1
  5.7 6.8 %collective-permute-start = (bf16[128,6144]{1,0:T(8,128)(2,1)S(1)}, bf16[128,6144]{1,0:T(8,128)(2,1)}, u32[]{:S(2)}, u32[]{:S(2)}) collective-permute-start(bf16[128,6144]{1,0:T(8,128)(2,1)S(1)} %fusion.4.x_ref), channel_id=1, source_target_pairs={{0,1},{1,2},{2,3},{4,5},{5,6},{6,7},{8,9},{9,10},{10,11},{12,13},{... | collective-permute-start | bytes 4718600 | tf_op jit(solution)/shard_map/ppermute | solution.py:110
  12.5 0.0 copy-done.10
  12.5 0.0 copy-done.11
  12.5 11.1 %project.4 = (bf16[128,768]{1,0:T(8,128)(2,1)S(1)}, bf16[2,128,768]{2,1,0:T(8,128)(2,1)S(1)}) custom-call(bf16[128,6144]{1,0:T(8,128)(2,1)S(1)} %fusion.4.x_ref, bf16[3,6144,768]{2,1,0:T(8,128)(2,1)} %w_ref.7, f32[1,768]{1,0:T(1,128)S(1)} %get-tuple-element.32.qg_ref, f32[1,768]{1,0:T(1,128)S(1)} %get-tuple-element.31.kg_ref), custom_call_target="tpu_custom_call" | custom-call | flops 3623878656 | bytes 28311552 | tf_op jit(solution)/shard_map/project/pallas_call | solution.py:31
  23.6 0.7 copy-done.4
  24.2 0.0 collective-permute-start.6
  24.2 19.6 %collective-permute-done.1 = bf16[128,6144]{1,0:T(8,128)(2,1)} collective-permute-done((bf16[128,6144]{1,0:T(8,128)(2,1)S(1)}, bf16[128,6144]{1,0:T(8,128)(2,1)}, u32[]{:S(2)}, u32[]{:S(2)}) %collective-permute-start.1) | collective-permute-done | bytes 1572896 | tf_op jit(solution)/shard_map/ppermute | solution.py:113
  43.9 1.3 collective-permute-start.3
  45.1 0.0 collective-permute-done
  45.2 0.8 collective-permute-start.2
  45.9 1.6 broadcast_select_fusion.1.x_ref
  47.5 11.0 %project.5 = (bf16[128,768]{1,0:T(8,128)(2,1)S(1)}, bf16[2,128,768]{2,1,0:T(8,128)(2,1)S(1)}) custom-call(bf16[128,6144]{1,0:T(8,128)(2,1)S(1)} %broadcast_select_fusion.1.x_ref, bf16[3,6144,768]{2,1,0:T(8,128)(2,1)} %w_ref.7, f32[1,768]{1,0:T(1,128)S(1)} %get-tuple-element.32.qg_ref, f32[1,768]{1,0:T(1,128)S(1)} %get-tuple-element.31.kg_ref), custom_call_target="tpu_custom_call" | custom-call | flops 3623878656 | bytes 28311552 | tf_op jit(solution)/shard_map/project/pallas_call | solution.py:31
  58.5 0.7 copy-done.5
  59.2 0.0 collective-permute-start.7
  59.2 22.3 %collective-permute-done.3 = bf16[128,6144]{1,0:T(8,128)(2,1)S(1)} collective-permute-done((bf16[128,6144]{1,0:T(8,128)(2,1)}, bf16[128,6144]{1,0:T(8,128)(2,1)S(1)}, u32[]{:S(2)}, u32[]{:S(2)}) %collective-permute-start.3) | collective-permute-done | bytes 1572896 | tf_op jit(solution)/shard_map/ppermute | solution.py:113
  81.5 1.3 collective-permute-start.5
  82.8 0.0 collective-permute-done.2
  82.8 0.9 collective-permute-start.4
  83.8 0.2 broadcast_select_fusion.x_ref
  83.9 11.0 %project.6 = (bf16[128,768]{1,0:T(8,128)(2,1)S(1)}, bf16[2,128,768]{2,1,0:T(8,128)(2,1)S(1)}) custom-call(bf16[128,6144]{1,0:T(8,128)(2,1)S(1)} %broadcast_select_fusion.x_ref, bf16[3,6144,768]{2,1,0:T(8,128)(2,1)} %w_ref.7, f32[1,768]{1,0:T(1,128)S(1)} %get-tuple-element.32.qg_ref, f32[1,768]{1,0:T(1,128)S(1)} %get-tuple-element.31.kg_ref), custom_call_target="tpu_custom_call" | custom-call | flops 3623878656 | bytes 28311552 | tf_op jit(solution)/shard_map/project/pallas_call | solution.py:31
  94.9 0.7 copy-done.6
  95.6 0.0 collective-permute-start.8
  95.6 22.5 %collective-permute-done.5 = bf16[128,6144]{1,0:T(8,128)(2,1)S(1)} collective-permute-done((bf16[128,6144]{1,0:T(8,128)(2,1)S(1)}, bf16[128,6144]{1,0:T(8,128)(2,1)S(1)}, u32[]{:S(2)}, u32[]{:S(2)}) %collective-permute-start.5) | collective-permute-done | bytes 1572896 | tf_op jit(solution)/shard_map/ppermute | solution.py:113
  118.1 0.0 collective-permute-done.4
  118.1 0.2 select_select_fusion.x_ref
  118.3 11.0 %project.7 = (bf16[128,768]{1,0:T(8,128)(2,1)S(1)}, bf16[2,128,768]{2,1,0:T(8,128)(2,1)S(1)}) custom-call(bf16[128,6144]{1,0:T(8,128)(2,1)S(1)} %select_select_fusion.x_ref, bf16[3,6144,768]{2,1,0:T(8,128)(2,1)} %w_ref.7, f32[1,768]{1,0:T(1,128)S(1)} %get-tuple-element.32.qg_ref, f32[1,768]{1,0:T(1,128)S(1)} %get-tuple-element.31.kg_ref), custom_call_target="tpu_custom_call" | custom-call | flops 3623878656 | bytes 28311552 | tf_op jit(solution)/shard_map/project/pallas_call | solution.py:31
  129.3 0.7 copy-done.7
  130.0 0.0 collective-permute-start.9
  130.0 0.0 collective-permute-done.6.refs_5_
  130.0 0.0 copy-start.12
  130.0 0.0 collective-permute-done.7.refs_7_
  130.0 0.0 collective-permute-done.8.refs_9_
  130.1 1.7 collective-permute-done.9.refs_11_
  131.7 0.7 copy-done.15
  132.5 11.8 %attend.1 = bf16[512,768]{1,0:T(8,128)(2,1)} custom-call(bf16[128,768]{1,0:T(8,128)(2,1)} %copy-done.4, bf16[128,768]{1,0:T(8,128)(2,1)} %copy-done.5, bf16[128,768]{1,0:T(8,128)(2,1)} %copy-done.6, bf16[128,768]{1,0:T(8,128)(2,1)} %copy-done.7, bf16[2,128,768]{2,1,0:T(8,128)(2,1)} %copy-done, bf16[2,128,768]{2,1,0:T(8,128)(2,1)} %copy-done.12, ...), custom_call_target="tpu_custom_call" | custom-call | flops 1610612736 | bytes 4718592 | tf_op jit(solution)/shard_map/attend/pallas_call | solution.py:78
  144.2 5.2 %convolution_convert_fusion = bf16[128,6144]{1,0:T(8,128)(2,1)S(1)} fusion(bf16[768,6144]{1,0:T(8,128)(2,1)} %param.11, bf16[512,768]{1,0:T(8,128)(2,1)} %attend.1, s32[]{:T(128)S(6)} %select_n.74), kind=kOutput, calls=%fused_computation | convolution fusion | flops 1208745984 | bytes 11206660 | tf_op jit(solution)/shard_map/dot_general | solution.py:159
  149.4 0.8 collective-permute-start.11
  150.2 4.1 %collective-permute-start.10 = (bf16[128,6144]{1,0:T(8,128)(2,1)S(1)}, bf16[128,6144]{1,0:T(8,128)(2,1)}, u32[]{:S(2)}, u32[]{:S(2)}) collective-permute-start(bf16[128,6144]{1,0:T(8,128)(2,1)S(1)} %convolution_convert_fusion), channel_id=1, source_target_pairs={{0,1},{4,5},{8,9},{12,13},{16,17},{20,21},{24,25},{28,29}} | collective-permute-start | bytes 4718600 | tf_op jit(solution)/shard_map/ppermute | solution.py:110
  154.2 5.2 %fusion.8 = f32[128,6144]{1,0:T(8,128)S(1)} fusion(bf16[768,6144]{1,0:T(8,128)(2,1)} %param.11, bf16[512,768]{1,0:T(8,128)(2,1)} %attend.1, s32[]{:T(128)S(6)} %select_n.72), kind=kOutput, calls=%fused_computation.18 | convolution fusion | flops 1207959552 | bytes 12779524 | tf_op jit(solution)/shard_map/dot_general | solution.py:159
  159.4 0.0 collective-permute-done.11
  159.5 27.5 %collective-permute-done.10 = bf16[128,6144]{1,0:T(8,128)(2,1)} collective-permute-done((bf16[128,6144]{1,0:T(8,128)(2,1)S(1)}, bf16[128,6144]{1,0:T(8,128)(2,1)}, u32[]{:S(2)}, u32[]{:S(2)}) %collective-permute-start.10) | collective-permute-done | bytes 1572896 | tf_op jit(solution)/shard_map/ppermute | solution.py:110
  187.0 3.2 %add_convert_fusion.3 = bf16[128,6144]{1,0:T(8,128)(2,1)} fusion(bf16[128,6144]{1,0:T(8,128)(2,1)S(1)} %collective-permute-done.11, f32[128,6144]{1,0:T(8,128)S(1)} %fusion.8, bf16[128,6144]{1,0:T(8,128)(2,1)} %collective-permute-done.10), kind=kLoop, calls=%fused_computation.11 | loop fusion | flops 3932160 | bytes 7864320 | tf_op jit(solution)/shard_map/convert_element_type | solution.py:170
  190.2 0.7 collective-permute-start.13
  191.0 0.0 slice-start.1
  191.0 0.0 slice-start.2
  191.0 5.3 %fusion.5 = f32[128,6144]{1,0:T(8,128)S(1)} fusion(bf16[768,6144]{1,0:T(8,128)(2,1)} %param.11, bf16[512,768]{1,0:T(8,128)(2,1)} %attend.1, s32[]{:T(128)S(6)} %select_n.75), kind=kOutput, calls=%fused_computation.15 | convolution fusion | flops 1207959552 | bytes 12779524 | tf_op jit(solution)/shard_map/dot_general | solution.py:159
  196.3 5.3 %collective-permute-start.12 = (bf16[128,6144]{1,0:T(8,128)(2,1)}, bf16[128,6144]{1,0:T(8,128)(2,1)S(1)}, u32[]{:S(2)}, u32[]{:S(2)}) collective-permute-start(bf16[128,6144]{1,0:T(8,128)(2,1)} %add_convert_fusion.3), channel_id=1, source_target_pairs={{0,1},{1,2},{4,5},{5,6},{8,9},{9,10},{12,13},{13,14},{16,17},{17,1... | collective-permute-start | bytes 4718600 | tf_op jit(solution)/shard_map/ppermute | solution.py:110
  201.7 2.3 fusion.10
  204.1 0.0 collective-permute-done.13
  204.1 1.6 add_convert_fusion.1
  205.6 29.1 %collective-permute-done.12 = bf16[128,6144]{1,0:T(8,128)(2,1)S(1)} collective-permute-done((bf16[128,6144]{1,0:T(8,128)(2,1)}, bf16[128,6144]{1,0:T(8,128)(2,1)S(1)}, u32[]{:S(2)}, u32[]{:S(2)}) %collective-permute-start.12) | collective-permute-done | bytes 1572896 | tf_op jit(solution)/shard_map/ppermute | solution.py:110
  234.8 0.3 add_convert_fusion.2
  235.1 6.7 %collective-permute-start.14 = (bf16[128,6144]{1,0:T(8,128)(2,1)S(1)}, bf16[128,6144]{1,0:T(8,128)(2,1)S(1)}, u32[]{:S(2)}, u32[]{:S(2)}) collective-permute-start(bf16[128,6144]{1,0:T(8,128)(2,1)S(1)} %add_convert_fusion.2), channel_id=1, source_target_pairs={{0,1},{1,2},{2,3},{4,5},{5,6},{6,7},{8,9},{9,10},{10,11},{12,13},{... | collective-permute-start | bytes 4718600 | tf_op jit(solution)/shard_map/ppermute | solution.py:110
  241.8 1.3 collective-permute-start.15
  243.2 5.2 %fusion.12 = f32[128,6144]{1,0:T(8,128)S(1)} fusion(bf16[768,6144]{1,0:T(8,128)(2,1)} %param.11, bf16[512,768]{1,0:T(8,128)(2,1)} %attend.1, s32[]{:T(128)S(6)} %select_n.70), kind=kOutput, calls=%fused_computation.22 | convolution fusion | flops 1207959552 | bytes 12779524 | tf_op jit(solution)/shard_map/dot_general | solution.py:159
  248.4 25.6 %collective-permute-done.14 = bf16[128,6144]{1,0:T(8,128)(2,1)S(1)} collective-permute-done((bf16[128,6144]{1,0:T(8,128)(2,1)S(1)}, bf16[128,6144]{1,0:T(8,128)(2,1)S(1)}, u32[]{:S(2)}, u32[]{:S(2)}) %collective-permute-start.14) | collective-permute-done | bytes 1572896 | tf_op jit(solution)/shard_map/ppermute | solution.py:110
  274.0 5.1 %collective-permute-done.15 = bf16[128,6144]{1,0:T(8,128)(2,1)} collective-permute-done((bf16[128,6144]{1,0:T(8,128)(2,1)}, bf16[128,6144]{1,0:T(8,128)(2,1)}, u32[]{:S(2)}, u32[]{:S(2)}) %collective-permute-start.15) | collective-permute-done | bytes 1572896 | tf_op jit(solution)/shard_map/ppermute | solution.py:113
  279.0 3.1 %add_convert_fusion = bf16[128,6144]{1,0:T(8,128)(2,1)} fusion(bf16[128,6144]{1,0:T(8,128)(2,1)} %collective-permute-done.15, f32[128,6144]{1,0:T(8,128)S(1)} %fusion.12, bf16[128,6144]{1,0:T(8,128)(2,1)S(1)} %collective-permute-done.14), kind=kLoop, calls=%fused_computation.8 | loop fusion | flops 3932160 | bytes 7864320 | tf_op jit(solution)/shard_map/convert_element_type | solution.py:184
  (30 shorter events, 0.1 us)
Async XLA Ops:
  0.0 3.8 %copy-start.8 = (bf16[128,6144]{1,0:T(8,128)(2,1)S(1)}, bf16[128,6144]{1,0:T(8,128)(2,1)}, u32[]{:S(2)}) copy-start(bf16[128,6144]{1,0:T(8,128)(2,1)} %param.6) | copy-start | bytes 4718596
  0.0 3.8 %copy-start.9 = (f32[6144]{0:T(1024)S(1)}, f32[6144]{0:T(1024)}, u32[]{:S(2)}) copy-start(f32[6144]{0:T(1024)} %param.7) | copy-start | bytes 73732
  0.0 12.5 %copy-start.10 = (f32[6,128]{1,0:T(8,128)S(1)}, f32[6,128]{1,0:T(8,128)}, u32[]{:S(2)}) copy-start(f32[6,128]{1,0:T(8,128)} %param.10) | copy-start | bytes 9220
  0.0 12.5 %copy-start.11 = (f32[6,128]{1,0:T(8,128)S(1)}, f32[6,128]{1,0:T(8,128)}, u32[]{:S(2)}) copy-start(f32[6,128]{1,0:T(8,128)} %param.9) | copy-start | bytes 9220
  4.4 39.5 %collective-permute-start.1 = (bf16[128,6144]{1,0:T(8,128)(2,1)S(1)}, bf16[128,6144]{1,0:T(8,128)(2,1)}, u32[]{:S(2)}, u32[]{:S(2)}) collective-permute-start(bf16[128,6144]{1,0:T(8,128)(2,1)S(1)} %fusion.4.x_ref), channel_id=1, source_target_pairs={{3,2},{2,1},{1,0},{7,6},{6,5},{5,4},{11,10},{10,9},{9,8},{15,14},{... | collective-permute-start | bytes 4718600 | tf_op jit(solution)/shard_map/ppermute | solution.py:113
  5.7 39.5 %collective-permute-start = (bf16[128,6144]{1,0:T(8,128)(2,1)S(1)}, bf16[128,6144]{1,0:T(8,128)(2,1)}, u32[]{:S(2)}, u32[]{:S(2)}) collective-permute-start(bf16[128,6144]{1,0:T(8,128)(2,1)S(1)} %fusion.4.x_ref), channel_id=1, source_target_pairs={{0,1},{1,2},{2,3},{4,5},{5,6},{6,7},{8,9},{9,10},{10,11},{12,13},{... | collective-permute-start | bytes 4718600 | tf_op jit(solution)/shard_map/ppermute | solution.py:110
  23.6 0.7 copy-start.4
  24.2 34.3 %copy-start = (bf16[2,128,768]{2,1,0:T(8,128)(2,1)}, bf16[2,128,768]{2,1,0:T(8,128)(2,1)S(1)}, u32[]{:S(2)}) copy-start(bf16[2,128,768]{2,1,0:T(8,128)(2,1)S(1)} %get-tuple-element.25.refs_4_) | copy-start | bytes 1179652
  24.2 105.7 %collective-permute-start.6 = (bf16[2,128,768]{2,1,0:T(8,128)(2,1)S(1)}, bf16[2,128,768]{2,1,0:T(8,128)(2,1)S(1)}, u32[]{:S(2)}, u32[]{:S(2)}) collective-permute-start(bf16[2,128,768]{2,1,0:T(8,128)(2,1)S(1)} %get-tuple-element.25.refs_4_), channel_id=1, source_target_pairs={{0,4},{4,0},{1,5},{5,1},{2,6},{6,2},{3,7},{7,3},{8,12},{12,8},{9,1... | collective-permute-start | bytes 1179656 | tf_op jit(solution)/shard_map/ppermute | solution.py:152
  43.9 37.7 %collective-permute-start.3 = (bf16[128,6144]{1,0:T(8,128)(2,1)}, bf16[128,6144]{1,0:T(8,128)(2,1)S(1)}, u32[]{:S(2)}, u32[]{:S(2)}) collective-permute-start(bf16[128,6144]{1,0:T(8,128)(2,1)} %collective-permute-done.1), channel_id=1, source_target_pairs={{2,1},{1,0},{6,5},{5,4},{10,9},{9,8},{14,13},{13,12},{18,17},{17,1... | collective-permute-start | bytes 4718600 | tf_op jit(solution)/shard_map/ppermute | solution.py:113
  45.2 37.6 %collective-permute-start.2 = (bf16[128,6144]{1,0:T(8,128)(2,1)}, bf16[128,6144]{1,0:T(8,128)(2,1)S(1)}, u32[]{:S(2)}, u32[]{:S(2)}) collective-permute-start(bf16[128,6144]{1,0:T(8,128)(2,1)} %collective-permute-done), channel_id=1, source_target_pairs={{1,2},{2,3},{5,6},{6,7},{9,10},{10,11},{13,14},{14,15},{17,18},{18... | collective-permute-start | bytes 4718600 | tf_op jit(solution)/shard_map/ppermute | solution.py:110
  58.5 0.7 copy-start.5
  59.2 35.7 %copy-start.1 = (bf16[2,128,768]{2,1,0:T(8,128)(2,1)}, bf16[2,128,768]{2,1,0:T(8,128)(2,1)S(1)}, u32[]{:S(2)}) copy-start(bf16[2,128,768]{2,1,0:T(8,128)(2,1)S(1)} %get-tuple-element.26.refs_6_) | copy-start | bytes 1179652
  59.2 70.8 %collective-permute-start.7 = (bf16[2,128,768]{2,1,0:T(8,128)(2,1)S(1)}, bf16[2,128,768]{2,1,0:T(8,128)(2,1)S(1)}, u32[]{:S(2)}, u32[]{:S(2)}) collective-permute-start(bf16[2,128,768]{2,1,0:T(8,128)(2,1)S(1)} %get-tuple-element.26.refs_6_), channel_id=1, source_target_pairs={{0,4},{4,0},{1,5},{5,1},{2,6},{6,2},{3,7},{7,3},{8,12},{12,8},{9,1... | collective-permute-start | bytes 1179656 | tf_op jit(solution)/shard_map/ppermute | solution.py:152
  81.5 36.6 %collective-permute-start.5 = (bf16[128,6144]{1,0:T(8,128)(2,1)S(1)}, bf16[128,6144]{1,0:T(8,128)(2,1)S(1)}, u32[]{:S(2)}, u32[]{:S(2)}) collective-permute-start(bf16[128,6144]{1,0:T(8,128)(2,1)S(1)} %collective-permute-done.3), channel_id=1, source_target_pairs={{1,0},{5,4},{9,8},{13,12},{17,16},{21,20},{25,24},{29,28}} | collective-permute-start | bytes 4718600 | tf_op jit(solution)/shard_map/ppermute | solution.py:113
  82.8 35.3 %collective-permute-start.4 = (bf16[128,6144]{1,0:T(8,128)(2,1)S(1)}, bf16[128,6144]{1,0:T(8,128)(2,1)S(1)}, u32[]{:S(2)}, u32[]{:S(2)}) collective-permute-start(bf16[128,6144]{1,0:T(8,128)(2,1)S(1)} %collective-permute-done.2), channel_id=1, source_target_pairs={{2,3},{6,7},{10,11},{14,15},{18,19},{22,23},{26,27},{30,31}} | collective-permute-start | bytes 4718600 | tf_op jit(solution)/shard_map/ppermute | solution.py:110
  94.9 0.7 copy-start.6
  95.6 22.7 %copy-start.2 = (bf16[2,128,768]{2,1,0:T(8,128)(2,1)}, bf16[2,128,768]{2,1,0:T(8,128)(2,1)S(1)}, u32[]{:S(2)}) copy-start(bf16[2,128,768]{2,1,0:T(8,128)(2,1)S(1)} %get-tuple-element.27.refs_8_) | copy-start | bytes 1179652
  95.6 34.4 %collective-permute-start.8 = (bf16[2,128,768]{2,1,0:T(8,128)(2,1)S(1)}, bf16[2,128,768]{2,1,0:T(8,128)(2,1)S(1)}, u32[]{:S(2)}, u32[]{:S(2)}) collective-permute-start(bf16[2,128,768]{2,1,0:T(8,128)(2,1)S(1)} %get-tuple-element.27.refs_8_), channel_id=1, source_target_pairs={{0,4},{4,0},{1,5},{5,1},{2,6},{6,2},{3,7},{7,3},{8,12},{12,8},{9,1... | collective-permute-start | bytes 1179656 | tf_op jit(solution)/shard_map/ppermute | solution.py:152
  129.3 0.7 copy-start.7
  130.0 1.7 copy-start.3
  130.0 1.7 collective-permute-start.9
  130.0 1.7 copy-start.12
  130.0 1.7 copy-start.13
  130.0 1.7 copy-start.14
  131.7 0.7 copy-start.15
  149.4 10.0 %collective-permute-start.11 = (bf16[128,6144]{1,0:T(8,128)(2,1)S(1)}, bf16[128,6144]{1,0:T(8,128)(2,1)S(1)}, u32[]{:S(2)}, u32[]{:S(2)}) collective-permute-start(bf16[128,6144]{1,0:T(8,128)(2,1)S(1)} %convolution_convert_fusion), channel_id=1, source_target_pairs={{3,2},{7,6},{11,10},{15,14},{19,18},{23,22},{27,26},{31,30}} | collective-permute-start | bytes 4718600 | tf_op jit(solution)/shard_map/ppermute | solution.py:113
  150.2 36.8 %collective-permute-start.10 = (bf16[128,6144]{1,0:T(8,128)(2,1)S(1)}, bf16[128,6144]{1,0:T(8,128)(2,1)}, u32[]{:S(2)}, u32[]{:S(2)}) collective-permute-start(bf16[128,6144]{1,0:T(8,128)(2,1)S(1)} %convolution_convert_fusion), channel_id=1, source_target_pairs={{0,1},{4,5},{8,9},{12,13},{16,17},{20,21},{24,25},{28,29}} | collective-permute-start | bytes 4718600 | tf_op jit(solution)/shard_map/ppermute | solution.py:110
  187.0 14.7 %slice-start = ((s8[9437184]{0:T(1024)(128)(4,1)}), s8[1048576]{0:T(1024)(128)(4,1)S(1)}, s32[]{:S(2)}) async-start(s8[9437184]{0:T(1024)(128)(4,1)} %bitcast.13), calls=%async_computation | async-start | bytes 2097152
  190.2 13.9 %collective-permute-start.13 = (bf16[128,6144]{1,0:T(8,128)(2,1)}, bf16[128,6144]{1,0:T(8,128)(2,1)S(1)}, u32[]{:S(2)}, u32[]{:S(2)}) collective-permute-start(bf16[128,6144]{1,0:T(8,128)(2,1)} %add_convert_fusion.3), channel_id=1, source_target_pairs={{3,2},{2,1},{7,6},{6,5},{11,10},{10,9},{15,14},{14,13},{19,18},{18... | collective-permute-start | bytes 4718600 | tf_op jit(solution)/shard_map/ppermute | solution.py:113
  191.0 10.7 %slice-start.1 = ((s8[9437184]{0:T(1024)(128)(4,1)}), s8[4194304]{0:T(1024)(128)(4,1)S(1)}, s32[]{:S(2)}) async-start(s8[9437184]{0:T(1024)(128)(4,1)} %bitcast.13), calls=%async_computation.1 | async-start | bytes 8388608
  191.0 10.7 %slice-start.2 = ((s8[9437184]{0:T(1024)(128)(4,1)}), s8[4194304]{0:T(1024)(128)(4,1)S(1)}, s32[]{:S(2)}) async-start(s8[9437184]{0:T(1024)(128)(4,1)} %bitcast.13), calls=%async_computation.2 | async-start | bytes 8388608
  196.3 38.4 %collective-permute-start.12 = (bf16[128,6144]{1,0:T(8,128)(2,1)}, bf16[128,6144]{1,0:T(8,128)(2,1)S(1)}, u32[]{:S(2)}, u32[]{:S(2)}) collective-permute-start(bf16[128,6144]{1,0:T(8,128)(2,1)} %add_convert_fusion.3), channel_id=1, source_target_pairs={{0,1},{1,2},{4,5},{5,6},{8,9},{9,10},{12,13},{13,14},{16,17},{17,1... | collective-permute-start | bytes 4718600 | tf_op jit(solution)/shard_map/ppermute | solution.py:110
  235.1 38.9 %collective-permute-start.14 = (bf16[128,6144]{1,0:T(8,128)(2,1)S(1)}, bf16[128,6144]{1,0:T(8,128)(2,1)S(1)}, u32[]{:S(2)}, u32[]{:S(2)}) collective-permute-start(bf16[128,6144]{1,0:T(8,128)(2,1)S(1)} %add_convert_fusion.2), channel_id=1, source_target_pairs={{0,1},{1,2},{2,3},{4,5},{5,6},{6,7},{8,9},{9,10},{10,11},{12,13},{... | collective-permute-start | bytes 4718600 | tf_op jit(solution)/shard_map/ppermute | solution.py:110
  241.8 37.2 %collective-permute-start.15 = (bf16[128,6144]{1,0:T(8,128)(2,1)}, bf16[128,6144]{1,0:T(8,128)(2,1)}, u32[]{:S(2)}, u32[]{:S(2)}) collective-permute-start(bf16[128,6144]{1,0:T(8,128)(2,1)} %add_convert_fusion.1), channel_id=1, source_target_pairs={{3,2},{2,1},{1,0},{7,6},{6,5},{5,4},{11,10},{10,9},{9,8},{15,14},{... | collective-permute-start | bytes 4718600 | tf_op jit(solution)/shard_map/ppermute | solution.py:113

commit v4 on v3

--- a/solution.py
+++ b/solution.py
@@ -57,11 +57,13 @@
     query_refs, kv_refs, out_ref = refs[:n_queries], refs[n_queries:-1], refs[-1]
     keys = jnp.concatenate([ref[0] for ref in kv_refs], axis=0)
     values = jnp.concatenate([ref[1] for ref in kv_refs], axis=0)
-    rows = query_refs[0].shape[0]
-    for number, ref in enumerate(query_refs):
+    pair = 2 if n_queries % 2 == 0 else 1
+    rows = query_refs[0].shape[0] * pair
+    for number in range(n_queries // pair):
+        group = [ref[...] for ref in query_refs[number * pair : (number + 1) * pair]]
         scores = (
             lax.dot_general(
-                ref[...], keys, (((1,), (1,)), ((), ())), preferred_element_type=jnp.float32
+                jnp.concatenate(group, axis=0), keys, (((1,), (1,)), ((), ())), preferred_element_type=jnp.float32
             )
             * scaling
         )

time: 283 us -> 280 us (0.989)
  no operation moved by 1% of the time
where the time goes in v4:
time: 280 us
  waiting for transfers between devices  154 us (55%)
  Pallas kernels  53.2 us (19%)
  starting transfers between devices  30.9 us (11%)
  matrix products  23.3 us (8%)
  other arithmetic  14.5 us (5%)
  local copies, waits for them, and re-layouts  3.49 us (1%)
    ppermute x6, waiting for transfers between devices, rightward(): lax.ppermute(value, 'stream', [(i, i + 1) for i in range(first, last)])  82.5 us
    ppermute x6, waiting for transfers between devices, leftward(): lax.ppermute(value, 'stream', [(i, i - 1) for i in range(first, last, -1)])  69.7 us
    pallas_call x4, Pallas kernels, project(): pl.pallas_call(functools.partial(project_kernel, head_size), grid=(width...  44 us
    ppermute x6, starting transfers between devices, rightward(): lax.ppermute(value, 'stream', [(i, i + 1) for i in range(first, last)])  24 us
    dot_general x5, matrix products, share(): return jnp.dot(piece, out_weight, preferred_element_type=jnp.float32)  23.3 us
    pallas_call x1, Pallas kernels, attend(): pl.pallas_call(functools.partial(attend_kernel, len(queries), scaling), g...  9.16 us
    ppermute x6, starting transfers between devices, leftward(): lax.ppermute(value, 'stream', [(i, i - 1) for i in range(first, last, -1)])  6.84 us
  transfers between devices with their start and end apart: 16, of which 8 were waited for; matrix products, arithmetic and copies ran while one was open for 8% of the time, Pallas kernels for 16%

profile of v4, /device:TPU:0, one launch (start us, length us, event | category | flops | bytes accessed | tf_op | source)
XLA Modules:
  0.0 279.5 jit_solution(7003681042511575005)
XLA Ops:
  0.0 1.8 convert_reduce_fusion
  1.8 2.0 fusion.2
  3.8 0.0 copy-done.8
  3.8 0.6 fusion.4.x_ref
  4.4 1.3 collective-permute-start.1
  5.7 6.8 %collective-permute-start = (bf16[128,6144]{1,0:T(8,128)(2,1)S(1)}, bf16[128,6144]{1,0:T(8,128)(2,1)}, u32[]{:S(2)}, u32[]{:S(2)}) collective-permute-start(bf16[128,6144]{1,0:T(8,128)(2,1)S(1)} %fusion.4.x_ref), channel_id=1, source_target_pairs={{0,1},{1,2},{2,3},{4,5},{5,6},{6,7},{8,9},{9,10},{10,11},{12,13},{... | collective-permute-start | bytes 4718600 | tf_op jit(solution)/shard_map/ppermute | solution.py:112
  12.5 0.0 copy-done.10
  12.5 11.1 %project.4 = (bf16[128,768]{1,0:T(8,128)(2,1)S(1)}, bf16[2,128,768]{2,1,0:T(8,128)(2,1)S(1)}) custom-call(bf16[128,6144]{1,0:T(8,128)(2,1)S(1)} %fusion.4.x_ref, bf16[3,6144,768]{2,1,0:T(8,128)(2,1)} %w_ref.7, f32[1,768]{1,0:T(1,128)S(1)} %get-tuple-element.32.qg_ref, f32[1,768]{1,0:T(1,128)S(1)} %get-tuple-element.31.kg_ref), custom_call_target="tpu_custom_call" | custom-call | flops 3623878656 | bytes 28311552 | tf_op jit(solution)/shard_map/project/pallas_call | solution.py:31
  23.6 0.7 copy-done.4
  24.2 0.0 collective-permute-start.6
  24.2 19.6 %collective-permute-done.1 = bf16[128,6144]{1,0:T(8,128)(2,1)} collective-permute-done((bf16[128,6144]{1,0:T(8,128)(2,1)S(1)}, bf16[128,6144]{1,0:T(8,128)(2,1)}, u32[]{:S(2)}, u32[]{:S(2)}) %collective-permute-start.1) | collective-permute-done | bytes 1572896 | tf_op jit(solution)/shard_map/ppermute | solution.py:115
  43.9 1.3 collective-permute-start.3
  45.1 0.0 collective-permute-done
  45.2 0.8 collective-permute-start.2
  45.9 1.6 broadcast_select_fusion.1.x_ref
  47.5 11.0 %project.5 = (bf16[128,768]{1,0:T(8,128)(2,1)S(1)}, bf16[2,128,768]{2,1,0:T(8,128)(2,1)S(1)}) custom-call(bf16[128,6144]{1,0:T(8,128)(2,1)S(1)} %broadcast_select_fusion.1.x_ref, bf16[3,6144,768]{2,1,0:T(8,128)(2,1)} %w_ref.7, f32[1,768]{1,0:T(1,128)S(1)} %get-tuple-element.32.qg_ref, f32[1,768]{1,0:T(1,128)S(1)} %get-tuple-element.31.kg_ref), custom_call_target="tpu_custom_call" | custom-call | flops 3623878656 | bytes 28311552 | tf_op jit(solution)/shard_map/project/pallas_call | solution.py:31
  58.5 0.7 copy-done.5
  59.2 0.0 collective-permute-start.7
  59.2 22.3 %collective-permute-done.3 = bf16[128,6144]{1,0:T(8,128)(2,1)S(1)} collective-permute-done((bf16[128,6144]{1,0:T(8,128)(2,1)}, bf16[128,6144]{1,0:T(8,128)(2,1)S(1)}, u32[]{:S(2)}, u32[]{:S(2)}) %collective-permute-start.3) | collective-permute-done | bytes 1572896 | tf_op jit(solution)/shard_map/ppermute | solution.py:115
  81.5 1.3 collective-permute-start.5
  82.8 0.0 collective-permute-done.2
  82.8 0.8 collective-permute-start.4
  83.6 0.2 broadcast_select_fusion.x_ref
  83.8 11.0 %project.6 = (bf16[128,768]{1,0:T(8,128)(2,1)S(1)}, bf16[2,128,768]{2,1,0:T(8,128)(2,1)S(1)}) custom-call(bf16[128,6144]{1,0:T(8,128)(2,1)S(1)} %broadcast_select_fusion.x_ref, bf16[3,6144,768]{2,1,0:T(8,128)(2,1)} %w_ref.7, f32[1,768]{1,0:T(1,128)S(1)} %get-tuple-element.32.qg_ref, f32[1,768]{1,0:T(1,128)S(1)} %get-tuple-element.31.kg_ref), custom_call_target="tpu_custom_call" | custom-call | flops 3623878656 | bytes 28311552 | tf_op jit(solution)/shard_map/project/pallas_call | solution.py:31
  94.8 0.7 copy-done.6
  95.4 0.0 collective-permute-start.8
  95.4 22.7 %collective-permute-done.5 = bf16[128,6144]{1,0:T(8,128)(2,1)S(1)} collective-permute-done((bf16[128,6144]{1,0:T(8,128)(2,1)S(1)}, bf16[128,6144]{1,0:T(8,128)(2,1)S(1)}, u32[]{:S(2)}, u32[]{:S(2)}) %collective-permute-start.5) | collective-permute-done | bytes 1572896 | tf_op jit(solution)/shard_map/ppermute | solution.py:115
  118.1 0.0 collective-permute-done.4
  118.1 0.2 select_select_fusion.x_ref
  118.3 11.0 %project.7 = (bf16[128,768]{1,0:T(8,128)(2,1)S(1)}, bf16[2,128,768]{2,1,0:T(8,128)(2,1)S(1)}) custom-call(bf16[128,6144]{1,0:T(8,128)(2,1)S(1)} %select_select_fusion.x_ref, bf16[3,6144,768]{2,1,0:T(8,128)(2,1)} %w_ref.7, f32[1,768]{1,0:T(1,128)S(1)} %get-tuple-element.32.qg_ref, f32[1,768]{1,0:T(1,128)S(1)} %get-tuple-element.31.kg_ref), custom_call_target="tpu_custom_call" | custom-call | flops 3623878656 | bytes 28311552 | tf_op jit(solution)/shard_map/project/pallas_call | solution.py:31
  129.3 0.7 copy-done.7
  130.0 0.0 collective-permute-start.9
  130.0 0.0 collective-permute-done.6.refs_5_
  130.0 0.0 copy-start.12
  130.0 0.0 collective-permute-done.7.refs_7_
  130.0 0.0 collective-permute-done.8.refs_9_
  130.1 1.7 collective-permute-done.9.refs_11_
  131.7 0.7 copy-done.15
  132.5 9.2 %attend.1 = bf16[512,768]{1,0:T(8,128)(2,1)} custom-call(bf16[128,768]{1,0:T(8,128)(2,1)} %copy-done.4, bf16[128,768]{1,0:T(8,128)(2,1)} %copy-done.5, bf16[128,768]{1,0:T(8,128)(2,1)} %copy-done.6, bf16[128,768]{1,0:T(8,128)(2,1)} %copy-done.7, bf16[2,128,768]{2,1,0:T(8,128)(2,1)} %copy-done, bf16[2,128,768]{2,1,0:T(8,128)(2,1)} %copy-done.12, ...), custom_call_target="tpu_custom_call" | custom-call | flops 1610612736 | bytes 4718592 | tf_op jit(solution)/shard_map/attend/pallas_call | solution.py:80
  141.6 5.2 %convolution_convert_fusion = bf16[128,6144]{1,0:T(8,128)(2,1)S(1)} fusion(bf16[768,6144]{1,0:T(8,128)(2,1)} %param.11, bf16[512,768]{1,0:T(8,128)(2,1)} %attend.1, s32[]{:T(128)S(6)} %select_n.74), kind=kOutput, calls=%fused_computation | convolution fusion | flops 1208745984 | bytes 11206660 | tf_op jit(solution)/shard_map/dot_general | solution.py:161
  146.8 0.9 collective-permute-start.11
  147.8 4.1 %collective-permute-start.10 = (bf16[128,6144]{1,0:T(8,128)(2,1)S(1)}, bf16[128,6144]{1,0:T(8,128)(2,1)}, u32[]{:S(2)}, u32[]{:S(2)}) collective-permute-start(bf16[128,6144]{1,0:T(8,128)(2,1)S(1)} %convolution_convert_fusion), channel_id=1, source_target_pairs={{0,1},{4,5},{8,9},{12,13},{16,17},{20,21},{24,25},{28,29}} | collective-permute-start | bytes 4718600 | tf_op jit(solution)/shard_map/ppermute | solution.py:112
  151.8 5.2 %fusion.8 = f32[128,6144]{1,0:T(8,128)S(1)} fusion(bf16[768,6144]{1,0:T(8,128)(2,1)} %param.11, bf16[512,768]{1,0:T(8,128)(2,1)} %attend.1, s32[]{:T(128)S(6)} %select_n.72), kind=kOutput, calls=%fused_computation.18 | convolution fusion | flops 1207959552 | bytes 12779524 | tf_op jit(solution)/shard_map/dot_general | solution.py:161
  157.0 0.0 collective-permute-done.11
  157.0 27.5 %collective-permute-done.10 = bf16[128,6144]{1,0:T(8,128)(2,1)} collective-permute-done((bf16[128,6144]{1,0:T(8,128)(2,1)S(1)}, bf16[128,6144]{1,0:T(8,128)(2,1)}, u32[]{:S(2)}, u32[]{:S(2)}) %collective-permute-start.10) | collective-permute-done | bytes 1572896 | tf_op jit(solution)/shard_map/ppermute | solution.py:112
  184.6 3.2 %add_convert_fusion.3 = bf16[128,6144]{1,0:T(8,128)(2,1)} fusion(bf16[128,6144]{1,0:T(8,128)(2,1)S(1)} %collective-permute-done.11, f32[128,6144]{1,0:T(8,128)S(1)} %fusion.8, bf16[128,6144]{1,0:T(8,128)(2,1)} %collective-permute-done.10), kind=kLoop, calls=%fused_computation.11 | loop fusion | flops 3932160 | bytes 7864320 | tf_op jit(solution)/shard_map/convert_element_type | solution.py:172
  187.8 0.7 collective-permute-start.13
  188.6 0.0 slice-start.1
  188.6 0.0 slice-start.2
  188.6 5.3 %fusion.5 = f32[128,6144]{1,0:T(8,128)S(1)} fusion(bf16[768,6144]{1,0:T(8,128)(2,1)} %param.11, bf16[512,768]{1,0:T(8,128)(2,1)} %attend.1, s32[]{:T(128)S(6)} %select_n.75), kind=kOutput, calls=%fused_computation.15 | convolution fusion | flops 1207959552 | bytes 12779524 | tf_op jit(solution)/shard_map/dot_general | solution.py:161
  193.9 5.1 %collective-permute-start.12 = (bf16[128,6144]{1,0:T(8,128)(2,1)}, bf16[128,6144]{1,0:T(8,128)(2,1)S(1)}, u32[]{:S(2)}, u32[]{:S(2)}) collective-permute-start(bf16[128,6144]{1,0:T(8,128)(2,1)} %add_convert_fusion.3), channel_id=1, source_target_pairs={{0,1},{1,2},{4,5},{5,6},{8,9},{9,10},{12,13},{13,14},{16,17},{17,1... | collective-permute-start | bytes 4718600 | tf_op jit(solution)/shard_map/ppermute | solution.py:112
  199.0 0.0 slice-done
  199.1 0.0 slice-done.1
  199.1 2.3 fusion.10
  201.4 0.0 collective-permute-done.13
  201.4 1.6 add_convert_fusion.1
  203.0 29.3 %collective-permute-done.12 = bf16[128,6144]{1,0:T(8,128)(2,1)S(1)} collective-permute-done((bf16[128,6144]{1,0:T(8,128)(2,1)}, bf16[128,6144]{1,0:T(8,128)(2,1)S(1)}, u32[]{:S(2)}, u32[]{:S(2)}) %collective-permute-start.12) | collective-permute-done | bytes 1572896 | tf_op jit(solution)/shard_map/ppermute | solution.py:112
  232.3 0.3 add_convert_fusion.2
  232.7 6.6 %collective-permute-start.14 = (bf16[128,6144]{1,0:T(8,128)(2,1)S(1)}, bf16[128,6144]{1,0:T(8,128)(2,1)S(1)}, u32[]{:S(2)}, u32[]{:S(2)}) collective-permute-start(bf16[128,6144]{1,0:T(8,128)(2,1)S(1)} %add_convert_fusion.2), channel_id=1, source_target_pairs={{0,1},{1,2},{2,3},{4,5},{5,6},{6,7},{8,9},{9,10},{10,11},{12,13},{... | collective-permute-start | bytes 4718600 | tf_op jit(solution)/shard_map/ppermute | solution.py:112
  239.2 1.3 collective-permute-start.15
  240.6 5.2 %fusion.12 = f32[128,6144]{1,0:T(8,128)S(1)} fusion(bf16[768,6144]{1,0:T(8,128)(2,1)} %param.11, bf16[512,768]{1,0:T(8,128)(2,1)} %attend.1, s32[]{:T(128)S(6)} %select_n.70), kind=kOutput, calls=%fused_computation.22 | convolution fusion | flops 1207959552 | bytes 12779524 | tf_op jit(solution)/shard_map/dot_general | solution.py:161
  245.8 25.6 %collective-permute-done.14 = bf16[128,6144]{1,0:T(8,128)(2,1)S(1)} collective-permute-done((bf16[128,6144]{1,0:T(8,128)(2,1)S(1)}, bf16[128,6144]{1,0:T(8,128)(2,1)S(1)}, u32[]{:S(2)}, u32[]{:S(2)}) %collective-permute-start.14) | collective-permute-done | bytes 1572896 | tf_op jit(solution)/shard_map/ppermute | solution.py:112
  271.4 5.1 %collective-permute-done.15 = bf16[128,6144]{1,0:T(8,128)(2,1)} collective-permute-done((bf16[128,6144]{1,0:T(8,128)(2,1)}, bf16[128,6144]{1,0:T(8,128)(2,1)}, u32[]{:S(2)}, u32[]{:S(2)}) %collective-permute-start.15) | collective-permute-done | bytes 1572896 | tf_op jit(solution)/shard_map/ppermute | solution.py:115
  276.4 3.1 %add_convert_fusion = bf16[128,6144]{1,0:T(8,128)(2,1)} fusion(bf16[128,6144]{1,0:T(8,128)(2,1)} %collective-permute-done.15, f32[128,6144]{1,0:T(8,128)S(1)} %fusion.12, bf16[128,6144]{1,0:T(8,128)(2,1)S(1)} %collective-permute-done.14), kind=kLoop, calls=%fused_computation.8 | loop fusion | flops 3932160 | bytes 7864320 | tf_op jit(solution)/shard_map/convert_element_type | solution.py:186
  (30 shorter events, 0.1 us)
Async XLA Ops:
  0.0 3.8 %copy-start.8 = (bf16[128,6144]{1,0:T(8,128)(2,1)S(1)}, bf16[128,6144]{1,0:T(8,128)(2,1)}, u32[]{:S(2)}) copy-start(bf16[128,6144]{1,0:T(8,128)(2,1)} %param.6) | copy-start | bytes 4718596
  0.0 3.8 %copy-start.9 = (f32[6144]{0:T(1024)S(1)}, f32[6144]{0:T(1024)}, u32[]{:S(2)}) copy-start(f32[6144]{0:T(1024)} %param.7) | copy-start | bytes 73732
  0.0 12.5 %copy-start.10 = (f32[6,128]{1,0:T(8,128)S(1)}, f32[6,128]{1,0:T(8,128)}, u32[]{:S(2)}) copy-start(f32[6,128]{1,0:T(8,128)} %param.10) | copy-start | bytes 9220
  0.0 12.5 %copy-start.11 = (f32[6,128]{1,0:T(8,128)S(1)}, f32[6,128]{1,0:T(8,128)}, u32[]{:S(2)}) copy-start(f32[6,128]{1,0:T(8,128)} %param.9) | copy-start | bytes 9220
  4.4 39.5 %collective-permute-start.1 = (bf16[128,6144]{1,0:T(8,128)(2,1)S(1)}, bf16[128,6144]{1,0:T(8,128)(2,1)}, u32[]{:S(2)}, u32[]{:S(2)}) collective-permute-start(bf16[128,6144]{1,0:T(8,128)(2,1)S(1)} %fusion.4.x_ref), channel_id=1, source_target_pairs={{3,2},{2,1},{1,0},{7,6},{6,5},{5,4},{11,10},{10,9},{9,8},{15,14},{... | collective-permute-start | bytes 4718600 | tf_op jit(solution)/shard_map/ppermute | solution.py:115
  5.7 39.5 %collective-permute-start = (bf16[128,6144]{1,0:T(8,128)(2,1)S(1)}, bf16[128,6144]{1,0:T(8,128)(2,1)}, u32[]{:S(2)}, u32[]{:S(2)}) collective-permute-start(bf16[128,6144]{1,0:T(8,128)(2,1)S(1)} %fusion.4.x_ref), channel_id=1, source_target_pairs={{0,1},{1,2},{2,3},{4,5},{5,6},{6,7},{8,9},{9,10},{10,11},{12,13},{... | collective-permute-start | bytes 4718600 | tf_op jit(solution)/shard_map/ppermute | solution.py:112
  23.6 0.7 copy-start.4
  24.2 34.3 %copy-start = (bf16[2,128,768]{2,1,0:T(8,128)(2,1)}, bf16[2,128,768]{2,1,0:T(8,128)(2,1)S(1)}, u32[]{:S(2)}) copy-start(bf16[2,128,768]{2,1,0:T(8,128)(2,1)S(1)} %get-tuple-element.25.refs_4_) | copy-start | bytes 1179652
  24.2 105.7 %collective-permute-start.6 = (bf16[2,128,768]{2,1,0:T(8,128)(2,1)S(1)}, bf16[2,128,768]{2,1,0:T(8,128)(2,1)S(1)}, u32[]{:S(2)}, u32[]{:S(2)}) collective-permute-start(bf16[2,128,768]{2,1,0:T(8,128)(2,1)S(1)} %get-tuple-element.25.refs_4_), channel_id=1, source_target_pairs={{0,4},{4,0},{1,5},{5,1},{2,6},{6,2},{3,7},{7,3},{8,12},{12,8},{9,1... | collective-permute-start | bytes 1179656 | tf_op jit(solution)/shard_map/ppermute | solution.py:154
  43.9 37.7 %collective-permute-start.3 = (bf16[128,6144]{1,0:T(8,128)(2,1)}, bf16[128,6144]{1,0:T(8,128)(2,1)S(1)}, u32[]{:S(2)}, u32[]{:S(2)}) collective-permute-start(bf16[128,6144]{1,0:T(8,128)(2,1)} %collective-permute-done.1), channel_id=1, source_target_pairs={{2,1},{1,0},{6,5},{5,4},{10,9},{9,8},{14,13},{13,12},{18,17},{17,1... | collective-permute-start | bytes 4718600 | tf_op jit(solution)/shard_map/ppermute | solution.py:115
  45.2 37.6 %collective-permute-start.2 = (bf16[128,6144]{1,0:T(8,128)(2,1)}, bf16[128,6144]{1,0:T(8,128)(2,1)S(1)}, u32[]{:S(2)}, u32[]{:S(2)}) collective-permute-start(bf16[128,6144]{1,0:T(8,128)(2,1)} %collective-permute-done), channel_id=1, source_target_pairs={{1,2},{2,3},{5,6},{6,7},{9,10},{10,11},{13,14},{14,15},{17,18},{18... | collective-permute-start | bytes 4718600 | tf_op jit(solution)/shard_map/ppermute | solution.py:112
  58.5 0.7 copy-start.5
  59.2 35.5 %copy-start.1 = (bf16[2,128,768]{2,1,0:T(8,128)(2,1)}, bf16[2,128,768]{2,1,0:T(8,128)(2,1)S(1)}, u32[]{:S(2)}) copy-start(bf16[2,128,768]{2,1,0:T(8,128)(2,1)S(1)} %get-tuple-element.26.refs_6_) | copy-start | bytes 1179652
  59.2 70.8 %collective-permute-start.7 = (bf16[2,128,768]{2,1,0:T(8,128)(2,1)S(1)}, bf16[2,128,768]{2,1,0:T(8,128)(2,1)S(1)}, u32[]{:S(2)}, u32[]{:S(2)}) collective-permute-start(bf16[2,128,768]{2,1,0:T(8,128)(2,1)S(1)} %get-tuple-element.26.refs_6_), channel_id=1, source_target_pairs={{0,4},{4,0},{1,5},{5,1},{2,6},{6,2},{3,7},{7,3},{8,12},{12,8},{9,1... | collective-permute-start | bytes 1179656 | tf_op jit(solution)/shard_map/ppermute | solution.py:154
  81.5 36.6 %collective-permute-start.5 = (bf16[128,6144]{1,0:T(8,128)(2,1)S(1)}, bf16[128,6144]{1,0:T(8,128)(2,1)S(1)}, u32[]{:S(2)}, u32[]{:S(2)}) collective-permute-start(bf16[128,6144]{1,0:T(8,128)(2,1)S(1)} %collective-permute-done.3), channel_id=1, source_target_pairs={{1,0},{5,4},{9,8},{13,12},{17,16},{21,20},{25,24},{29,28}} | collective-permute-start | bytes 4718600 | tf_op jit(solution)/shard_map/ppermute | solution.py:115
  82.8 35.3 %collective-permute-start.4 = (bf16[128,6144]{1,0:T(8,128)(2,1)S(1)}, bf16[128,6144]{1,0:T(8,128)(2,1)S(1)}, u32[]{:S(2)}, u32[]{:S(2)}) collective-permute-start(bf16[128,6144]{1,0:T(8,128)(2,1)S(1)} %collective-permute-done.2), channel_id=1, source_target_pairs={{2,3},{6,7},{10,11},{14,15},{18,19},{22,23},{26,27},{30,31}} | collective-permute-start | bytes 4718600 | tf_op jit(solution)/shard_map/ppermute | solution.py:112
  94.7 0.7 copy-start.6
  95.4 22.9 %copy-start.2 = (bf16[2,128,768]{2,1,0:T(8,128)(2,1)}, bf16[2,128,768]{2,1,0:T(8,128)(2,1)S(1)}, u32[]{:S(2)}) copy-start(bf16[2,128,768]{2,1,0:T(8,128)(2,1)S(1)} %get-tuple-element.27.refs_8_) | copy-start | bytes 1179652
  95.4 34.6 %collective-permute-start.8 = (bf16[2,128,768]{2,1,0:T(8,128)(2,1)S(1)}, bf16[2,128,768]{2,1,0:T(8,128)(2,1)S(1)}, u32[]{:S(2)}, u32[]{:S(2)}) collective-permute-start(bf16[2,128,768]{2,1,0:T(8,128)(2,1)S(1)} %get-tuple-element.27.refs_8_), channel_id=1, source_target_pairs={{0,4},{4,0},{1,5},{5,1},{2,6},{6,2},{3,7},{7,3},{8,12},{12,8},{9,1... | collective-permute-start | bytes 1179656 | tf_op jit(solution)/shard_map/ppermute | solution.py:154
  129.3 0.7 copy-start.7
  130.0 1.7 copy-start.3
  130.0 1.7 collective-permute-start.9
  130.0 1.7 copy-start.12
  130.0 1.7 copy-start.13
  130.0 1.7 copy-start.14
  131.7 0.7 copy-start.15
  146.8 10.2 %collective-permute-start.11 = (bf16[128,6144]{1,0:T(8,128)(2,1)S(1)}, bf16[128,6144]{1,0:T(8,128)(2,1)S(1)}, u32[]{:S(2)}, u32[]{:S(2)}) collective-permute-start(bf16[128,6144]{1,0:T(8,128)(2,1)S(1)} %convolution_convert_fusion), channel_id=1, source_target_pairs={{3,2},{7,6},{11,10},{15,14},{19,18},{23,22},{27,26},{31,30}} | collective-permute-start | bytes 4718600 | tf_op jit(solution)/shard_map/ppermute | solution.py:115
  147.8 36.8 %collective-permute-start.10 = (bf16[128,6144]{1,0:T(8,128)(2,1)S(1)}, bf16[128,6144]{1,0:T(8,128)(2,1)}, u32[]{:S(2)}, u32[]{:S(2)}) collective-permute-start(bf16[128,6144]{1,0:T(8,128)(2,1)S(1)} %convolution_convert_fusion), channel_id=1, source_target_pairs={{0,1},{4,5},{8,9},{12,13},{16,17},{20,21},{24,25},{28,29}} | collective-permute-start | bytes 4718600 | tf_op jit(solution)/shard_map/ppermute | solution.py:112
  184.6 14.5 %slice-start = ((s8[9437184]{0:T(1024)(128)(4,1)}), s8[1048576]{0:T(1024)(128)(4,1)S(1)}, s32[]{:S(2)}) async-start(s8[9437184]{0:T(1024)(128)(4,1)} %bitcast.13), calls=%async_computation | async-start | bytes 2097152
  187.8 13.7 %collective-permute-start.13 = (bf16[128,6144]{1,0:T(8,128)(2,1)}, bf16[128,6144]{1,0:T(8,128)(2,1)S(1)}, u32[]{:S(2)}, u32[]{:S(2)}) collective-permute-start(bf16[128,6144]{1,0:T(8,128)(2,1)} %add_convert_fusion.3), channel_id=1, source_target_pairs={{3,2},{2,1},{7,6},{6,5},{11,10},{10,9},{15,14},{14,13},{19,18},{18... | collective-permute-start | bytes 4718600 | tf_op jit(solution)/shard_map/ppermute | solution.py:115
  188.6 10.5 %slice-start.1 = ((s8[9437184]{0:T(1024)(128)(4,1)}), s8[4194304]{0:T(1024)(128)(4,1)S(1)}, s32[]{:S(2)}) async-start(s8[9437184]{0:T(1024)(128)(4,1)} %bitcast.13), calls=%async_computation.1 | async-start | bytes 8388608
  188.6 10.5 %slice-start.2 = ((s8[9437184]{0:T(1024)(128)(4,1)}), s8[4194304]{0:T(1024)(128)(4,1)S(1)}, s32[]{:S(2)}) async-start(s8[9437184]{0:T(1024)(128)(4,1)} %bitcast.13), calls=%async_computation.2 | async-start | bytes 8388608
  193.9 38.4 %collective-permute-start.12 = (bf16[128,6144]{1,0:T(8,128)(2,1)}, bf16[128,6144]{1,0:T(8,128)(2,1)S(1)}, u32[]{:S(2)}, u32[]{:S(2)}) collective-permute-start(bf16[128,6144]{1,0:T(8,128)(2,1)} %add_convert_fusion.3), channel_id=1, source_target_pairs={{0,1},{1,2},{4,5},{5,6},{8,9},{9,10},{12,13},{13,14},{16,17},{17,1... | collective-permute-start | bytes 4718600 | tf_op jit(solution)/shard_map/ppermute | solution.py:112
  232.7 38.7 %collective-permute-start.14 = (bf16[128,6144]{1,0:T(8,128)(2,1)S(1)}, bf16[128,6144]{1,0:T(8,128)(2,1)S(1)}, u32[]{:S(2)}, u32[]{:S(2)}) collective-permute-start(bf16[128,6144]{1,0:T(8,128)(2,1)S(1)} %add_convert_fusion.2), channel_id=1, source_target_pairs={{0,1},{1,2},{2,3},{4,5},{5,6},{6,7},{8,9},{9,10},{10,11},{12,13},{... | collective-permute-start | bytes 4718600 | tf_op jit(solution)/shard_map/ppermute | solution.py:112
  239.2 37.2 %collective-permute-start.15 = (bf16[128,6144]{1,0:T(8,128)(2,1)}, bf16[128,6144]{1,0:T(8,128)(2,1)}, u32[]{:S(2)}, u32[]{:S(2)}) collective-permute-start(bf16[128,6144]{1,0:T(8,128)(2,1)} %add_convert_fusion.1), channel_id=1, source_target_pairs={{3,2},{2,1},{1,0},{7,6},{6,5},{5,4},{11,10},{10,9},{9,8},{15,14},{... | collective-permute-start | bytes 4718600 | tf_op jit(solution)/shard_map/ppermute | solution.py:115
